TPU v7x, 256 devices: a whole 4x4x8 slice. The times are simulated.
256 devices in a mesh: dp: 4 (over y), ep: 32 (over x, z), tp: 2 (over core).
Axes of the slice: x: 4, y: 4, z: 8, core: 2. Of those that a mesh axis runs over, the one named last changes fastest.
Arguments:
- grad_out: bfloat16 [16384, 4096], P(('dp', 'ep'), 'tp'), may hold values from -6 to 6
- hidden: bfloat16 [16384, 8, 768], P(('dp', 'ep'), None, 'tp'), may hold values from -0.29882812 to 0.29882812
- gates: bfloat16 [16384, 8], P(('dp', 'ep')), may hold values from 0.019897461 to 0.29882812
- expert_ids: int32 [16384, 8], P(('dp', 'ep')), may hold values from 0 to 63, all different within a row; in each aligned block of 128 rows (0 to 127, 128 to 255, ...) at most 24 rows name the same one
- down_weight: bfloat16 [64, 768, 4096], P('ep', 'tp'), may hold values from -0.09375 to 0.09375
Outputs:
- d_hidden: bfloat16 [16384, 8, 768], P(('dp', 'ep'), None, 'tp')
- d_gates: bfloat16 [16384, 8], P(('dp', 'ep'))
- d_weight: bfloat16 [64, 768, 4096], P('ep', 'tp', 'dp')
Inputs may be any that keep to these rules, and one draw needn't show every extreme that they name: `expert_ids`: in each aligned block of 128 rows (the tokens of one index of dp and ep taken together), no expert is named by more than 24 rows, a bound that some block reaches; the 8 experts of a token differ.
All inputs are finite; a program needn't handle non-finite values.
Results may differ from a plain program's by a relative error of at most 0.0049.
Values may be sent and summed in bfloat16 or wider, within the bound.
A program may use at most 256 MiB of HBM per device.

v0:
```python
import jax
import jax.numpy as jnp
from jax import lax
from jax.sharding import PartitionSpec as P


def shards(grad_out, hidden, gates, expert_ids, down_weight):
    ep_size = lax.axis_size("ep")
    experts_here, hidden_part, model_width = down_weight.shape
    experts_all = ep_size * experts_here
    tok_count, top_count = expert_ids.shape
    capacity = min(tok_count, 3 * tok_count * top_count // (2 * experts_all))
    pair_count = tok_count * top_count
    slot_count = experts_here * capacity
    flat_ids = expert_ids.reshape(pair_count)
    one_hot = (flat_ids[:, None] == jnp.arange(experts_all, dtype=jnp.int32)[None, :]).astype(
        jnp.int32
    )
    rank_in = jnp.sum((jnp.cumsum(one_hot, axis=0) - 1) * one_hot, axis=1)
    slot_of = flat_ids * capacity + rank_in
    source = (
        jnp.full((experts_all * capacity,), pair_count, jnp.int32)
        .at[slot_of]
        .set(jnp.arange(pair_count, dtype=jnp.int32))
    )
    filled = source < pair_count
    safe_idx = jnp.where(filled, source, 0)
    zero_half = jnp.zeros((), jnp.bfloat16)
    hid_rows = jnp.where(
        filled[:, None], hidden.reshape(pair_count, hidden_part)[safe_idx], zero_half
    ).reshape(ep_size, slot_count, hidden_part)
    gate_rows = jnp.where(filled, gates.reshape(pair_count)[safe_idx], zero_half).reshape(
        ep_size, slot_count
    )
    chosen = jnp.where(filled[:, None], grad_out[safe_idx // top_count], zero_half)
    half_recv = lax.all_to_all(
        chosen.reshape(ep_size, slot_count, grad_out.shape[1]),
        "ep",
        split_axis=0,
        concat_axis=0,
        tiled=True,
    )
    hid_recv = lax.all_to_all(hid_rows, "ep", split_axis=0, concat_axis=0, tiled=True)
    gate_recv = lax.all_to_all(gate_rows, "ep", split_axis=0, concat_axis=0, tiled=True)
    dy_recv = lax.all_gather(half_recv, "tp", axis=2, tiled=True)
    dy_slots = dy_recv.reshape(ep_size, experts_here, capacity, model_width)
    hid_slots = hid_recv.reshape(ep_size, experts_here, capacity, hidden_part)
    gate_slots = gate_recv.reshape(ep_size, experts_here, capacity).astype(jnp.float32)
    back_proj = jnp.einsum(
        "secd,efd->secf", dy_slots, down_weight, preferred_element_type=jnp.float32
    )
    partial_value = jnp.sum(back_proj * hid_slots.astype(jnp.float32), axis=3)
    dot_total = lax.psum(partial_value, "tp")
    send_dh = (
        (gate_slots[..., None] * back_proj)
        .astype(jnp.bfloat16)
        .reshape(ep_size, slot_count, hidden_part)
    )
    send_dg = dot_total.astype(jnp.bfloat16).reshape(ep_size, slot_count)
    got_dh, got_dg = (
        lax.all_to_all(send_dh, "ep", split_axis=0, concat_axis=0, tiled=True),
        lax.all_to_all(send_dg, "ep", split_axis=0, concat_axis=0, tiled=True),
    )
    d_hidden = got_dh.reshape(experts_all * capacity, hidden_part)[slot_of].reshape(
        tok_count, top_count, hidden_part
    )
    d_gates = got_dg.reshape(experts_all * capacity)[slot_of].reshape(tok_count, top_count)
    scaled = (gate_slots[..., None] * hid_slots.astype(jnp.float32)).astype(jnp.bfloat16)
    weight_term = jnp.einsum("secf,secd->efd", scaled, dy_slots, preferred_element_type=jnp.float32)
    d_weight = lax.psum_scatter(weight_term, "dp", scatter_dimension=2, tiled=True).astype(
        jnp.bfloat16
    )
    return (d_hidden, d_gates, d_weight)


def solution(mesh):
    placed = (
        P(("dp", "ep"), "tp"),
        P(("dp", "ep"), None, "tp"),
        P(("dp", "ep"), None),
        P(("dp", "ep"), None),
        P("ep", "tp", None),
    )
    return jax.shard_map(
        shards,
        mesh=mesh,
        in_specs=placed,
        out_specs=(P(("dp", "ep"), None, "tp"), P(("dp", "ep"), None), P("ep", "tp", "dp")),
        check_vma=False,
    )
```

profile of v0, /device:TPU:1, one launch (start us, length us, event | category | flops | bytes accessed | tf_op | source)
XLA Modules:
  0.0 393.1 jit_solution(15919698274863746796)
XLA Ops:
  7.2 0.9 copy.58
  8.1 0.1 eq.29
  8.2 0.1 eq.25
  8.3 0.7 broadcast_multiply_fusion
  9.0 18.0 %reduce-window.6 = s32[64,8,128]{2,1,0:T(8,128)S(1)} reduce-window(s32[64,8,128]{2,1,0:T(8,128)S(1)} %fusion.13, s32[]{:T(128)} %constant.28.clone.1), window={size=1x1x128 pad=0_0x0_0x127_0}, to_apply=%region_0.0 | reduce-window | flops 8323072 | bytes 524292 | tf_op jit(solution)/shard_map/reduce-window
  27.0 0.1 slice.18
  27.2 0.1 copy.60
  27.4 0.1 copy.61
  27.4 0.1 add_add_fusion
  27.6 0.1 copy.57
  27.7 0.1 mul.38
  27.8 0.1 fusion.12
  27.9 4.3 %scatter_custom_fusion = s32[1536]{0:T(1024)S(1)} fusion(s32[1024]{0:T(1024)S(1)} %bitcast.57, s32[1024]{0:T(1024)S(1)} %iota.11, s32[]{:T(128)} %constant.13.clone.1), kind=kCustom, calls=%fused_computation.40 | custom fusion | bytes 6148 | tf_op jit(solution)/shard_map/scatter | solution.py:24
  32.2 0.1 broadcast_in_dim.52
  32.4 7.1 %gather_fusion.1 = bf16[1536,2048]{1,0:T(8,128)(2,1)} fusion(bf16[128,2048]{1,0:T(8,128)(2,1)S(1)} %copy-done.1, s32[2048]{0:T(1024)S(1)} %pad_clamp_fusion), kind=kCustom, calls=%fused_computation.1 | custom fusion | bytes 12589056 | tf_op jit(solution)/shard_map/gather | solution.py:35
  39.4 3.3 broadcast_select_fusion
  42.7 148.4 %all_to_all.34 = bf16[32,48,2048]{2,1,0:T(8,128)(2,1)} all-to-all(bf16[32,48,2048]{2,1,0:T(8,128)(2,1)S(1)} %broadcast_select_fusion), channel_id=1, replica_groups=mesh['dp'=4,'ep'=32,'tp'=2] {'ep'}, dimensions={0} | all-to-all | bytes 12582912 | tf_op jit(solution)/shard_map/all_to_all | solution.py:36
  191.2 0.7 copy-done.2
  191.9 0.1 copy.62
  192.0 0.1 reshape.114
  192.1 9.5 %gather_fusion = bf16[1536]{0:T(1024)(128)(2,1)S(1)} fusion(bf16[1024]{0:T(1024)(128)(2,1)S(1)} %reshape.114, s32[2048]{0:T(1024)S(1)} %pad_clamp_fusion.1), kind=kCustom, calls=%fused_computation | custom fusion | bytes 12288 | tf_op jit(solution)/shard_map/gather | solution.py:32
  201.6 0.7 all_to_all.28
  202.3 8.8 %all-to-all-start = ((bf16[32,1,48]{2,1,0:T(2,128)(2,1)}), bf16[32,1,48]{2,1,0:T(2,128)(2,1)S(1)}, u32[]{:S(2)}, u32[]{:S(2)}) async-start(bf16[32,1,48]{2,1,0:T(2,128)(2,1)} %all_to_all.28), calls=%async_computation | async-start | bytes 32768 | tf_op jit(solution)/shard_map/all_to_all | solution.py:44
  211.1 4.7 %gather_fusion.3 = bf16[1536,384]{1,0:T(8,128)(2,1)S(1)} fusion(bf16[1024,384]{1,0:T(8,128)(2,1)S(1)} %bitcast.45, s32[2048]{0:T(1024)S(1)} %pad_clamp_fusion.1), kind=kCustom, calls=%fused_computation.3 | custom fusion | bytes 2365440 | tf_op jit(solution)/shard_map/gather | solution.py:30
  215.8 1.3 broadcast_select_fusion.1
  217.1 2.6 all-to-all-done
  219.7 6.7 %all-to-all-start.3 = ((bf16[32,48,384]{2,1,0:T(8,128)(2,1)}), bf16[32,48,384]{2,1,0:T(8,128)(2,1)S(1)}, u32[]{:S(2)}, u32[]{:S(2)}) async-start(bf16[32,48,384]{2,1,0:T(8,128)(2,1)} %broadcast_select_fusion.1), calls=%async_computation.3 | async-start | bytes 2359296 | tf_op jit(solution)/shard_map/all_to_all | solution.py:43
  226.4 0.2 reduce-scatter.2.cloned.1.call-start
  226.6 0.1 copy.64
  226.7 0.1 copy.65
  226.8 27.2 %all-to-all-done.3 = bf16[32,48,384]{2,1,0:T(8,128)(2,1)S(1)} async-done(((bf16[32,48,384]{2,1,0:T(8,128)(2,1)}), bf16[32,48,384]{2,1,0:T(8,128)(2,1)S(1)}, u32[]{:S(2)}, u32[]{:S(2)}) %all-to-all-start.3) | async-done | bytes 1179680 | tf_op jit(solution)/shard_map/all_to_all | solution.py:43
  254.0 11.0 %fusion.4 = f32[2,384,4096]{2,1,0:T(8,128)} fusion(bf16[32,2,24,4096]{3,2,1,0:T(8,128)(2,1)} %bitcast.59, f32[32,2,24]{2,0,1:T(8,128)S(1)} %copy.65, bf16[32,2,24,384]{3,2,1,0:T(8,128)(2,1)S(1)} %bitcast.49), kind=kOutput, calls=%fused_computation.10 | convolution fusion | flops 4833607680 | bytes 26351616 | tf_op jit(solution)/shard_map/secf,secd->efd/dot_general | solution.py:69
  265.0 11.7 %fusion.9 = (f32[32,2,24]{2,0,1:T(8,128)S(1)}, bf16[32,2,24,384]{3,2,0,1:T(8,128)(2,1)S(1)}) fusion(f32[32,2,24]{2,0,1:T(8,128)S(1)} %copy.65, bf16[2,384,4096]{2,1,0:T(8,128)(2,1)} %param.9, bf16[32,2,24,4096]{3,2,1,0:T(8,128)(2,1)} %bitcast.60, bf16[32,2,24,384]{3,2,1,0:T(8,128)(2,1)S(1)} %bitcast.50), kind=kOutput, calls=%fused_computation.16 | convolution fusion | flops 4834785792 | bytes 21245952 | tf_op jit(solution)/shard_map/secd,efd->secf/dot_general | solution.py:49
  276.7 0.1 copy.69
  276.7 8.0 %psum.7 = bf16[32,2,24]{0,2,1:T(8,128)(2,1)S(1)} all-reduce(f32[32,2,24]{0,2,1:T(8,128)S(1)} %copy.69), channel_id=1, replica_groups=mesh['dp'=4,'ep'=32,'tp'=2] {'tp'}, use_global_device_ids=true, to_apply=%region_5.6 | all-reduce | flops 1536 | bytes 9216 | tf_op jit(solution)/shard_map/psum | solution.py:53
  284.7 0.7 copy.70
  285.4 4.8 %all-to-all-start.4 = ((bf16[32,1,48]{2,1,0:T(2,128)(2,1)}), bf16[32,1,48]{2,1,0:T(2,128)(2,1)S(1)}, u32[]{:S(2)}, u32[]{:S(2)}) async-start(bf16[32,1,48]{2,1,0:T(2,128)(2,1)} %copy.70), calls=%async_computation.4 | async-start | bytes 32768 | tf_op jit(solution)/shard_map/all_to_all | solution.py:62
  290.3 1.1 copy.67
  291.4 7.5 %all-to-all-done.4 = bf16[32,1,48]{2,1,0:T(2,128)(2,1)S(1)} async-done(((bf16[32,1,48]{2,1,0:T(2,128)(2,1)}), bf16[32,1,48]{2,1,0:T(2,128)(2,1)S(1)}, u32[]{:S(2)}, u32[]{:S(2)}) %all-to-all-start.4) | async-done | bytes 3104 | tf_op jit(solution)/shard_map/all_to_all | solution.py:62
  298.9 3.9 %all-to-all-start.2 = ((bf16[32,48,384]{2,1,0:T(8,128)(2,1)}), bf16[32,48,384]{2,1,0:T(8,128)(2,1)S(1)}, u32[]{:S(2)}, u32[]{:S(2)}) async-start(bf16[32,48,384]{2,1,0:T(8,128)(2,1)} %bitcast.10), calls=%async_computation.2 | async-start | bytes 2359296 | tf_op jit(solution)/shard_map/all_to_all | solution.py:61
  302.9 0.1 reshape.120
  303.0 6.8 %gather_fusion.4 = bf16[1024]{0:T(1024)(128)(2,1)S(1)} fusion(bf16[1536]{0:T(1024)(128)(2,1)S(1)} %reshape.120, s32[1024]{0:T(1024)S(1)} %broadcast_clamp_fusion), kind=kCustom, calls=%fused_computation.4 | custom fusion | bytes 8192 | tf_op jit(solution)/shard_map/gather | solution.py:67
  309.8 0.1 reshape.121
  309.9 0.7 copy.73
  310.5 20.0 %all-to-all-done.2 = bf16[32,48,384]{2,1,0:T(8,128)(2,1)S(1)} async-done(((bf16[32,48,384]{2,1,0:T(8,128)(2,1)}), bf16[32,48,384]{2,1,0:T(8,128)(2,1)S(1)}, u32[]{:S(2)}, u32[]{:S(2)}) %all-to-all-start.2) | async-done | bytes 1179680 | tf_op jit(solution)/shard_map/all_to_all | solution.py:61
  330.6 5.0 %gather_fusion.2 = bf16[1024,384]{1,0:T(8,128)(2,1)} fusion(bf16[1536,384]{1,0:T(8,128)(2,1)S(1)} %bitcast.46, s32[1024]{0:T(1024)S(1)} %broadcast_clamp_fusion), kind=kCustom, calls=%fused_computation.2 | custom fusion | bytes 1576960 | tf_op jit(solution)/shard_map/gather | solution.py:64
  335.6 47.4 %reduce-scatter.2.cloned.1.call-done = f32[2,384,1024]{2,1,0:T(8,128)} async-done(((f32[2,384,4096]{2,1,0:T(8,128)}), f32[2,384,1024]{2,1,0:T(8,128)}) %reduce-scatter.2.cloned.1.call-update) | async-done | bytes 3145744 | tf_op jit(solution)/shard_map/reduce_scatter | solution.py:70
  383.0 3.3 convert_element_type.42
  (21 shorter events, 0.3 us)
Async XLA Ops:
  7.2 203.9 %copy-start = (bf16[128,8,384]{2,1,0:T(8,128)(2,1)S(1)}, bf16[128,8,384]{2,1,0:T(8,128)(2,1)}, u32[]{:S(2)}) copy-start(bf16[128,8,384]{2,1,0:T(8,128)(2,1)} %param.6) | copy-start | bytes 2359300
  7.2 25.2 %copy-start.1 = (bf16[128,2048]{1,0:T(8,128)(2,1)S(1)}, bf16[128,2048]{1,0:T(8,128)(2,1)}, u32[]{:S(2)}) copy-start(bf16[128,2048]{1,0:T(8,128)(2,1)} %param.5) | copy-start | bytes 1572868
  7.2 246.8 %all-gather.2.cloned.1.call-start = ((), (), s32[]{:S(2)}) async-start(), calls=%async_computation.6 | async-start | bytes 18874368 | tf_op jit(solution)/shard_map/all_gather | solution.py:45
  191.2 0.7 copy-start.2
  202.3 17.4 %all-to-all-start = ((bf16[32,1,48]{2,1,0:T(2,128)(2,1)}), bf16[32,1,48]{2,1,0:T(2,128)(2,1)S(1)}, u32[]{:S(2)}, u32[]{:S(2)}) async-start(bf16[32,1,48]{2,1,0:T(2,128)(2,1)} %all_to_all.28), calls=%async_computation | async-start | bytes 32768 | tf_op jit(solution)/shard_map/all_to_all | solution.py:44
  219.7 34.3 %all-to-all-start.3 = ((bf16[32,48,384]{2,1,0:T(8,128)(2,1)}), bf16[32,48,384]{2,1,0:T(8,128)(2,1)S(1)}, u32[]{:S(2)}, u32[]{:S(2)}) async-start(bf16[32,48,384]{2,1,0:T(8,128)(2,1)} %broadcast_select_fusion.1), calls=%async_computation.3 | async-start | bytes 2359296 | tf_op jit(solution)/shard_map/all_to_all | solution.py:43
  226.4 156.6 %reduce-scatter.2.cloned.1.call-start = ((), (), s32[]{:S(2)}) async-start(), calls=%async_computation.7 | async-start | bytes 15728640 | tf_op jit(solution)/shard_map/reduce_scatter | solution.py:70
  285.4 13.4 %all-to-all-start.4 = ((bf16[32,1,48]{2,1,0:T(2,128)(2,1)}), bf16[32,1,48]{2,1,0:T(2,128)(2,1)S(1)}, u32[]{:S(2)}, u32[]{:S(2)}) async-start(bf16[32,1,48]{2,1,0:T(2,128)(2,1)} %copy.70), calls=%async_computation.4 | async-start | bytes 32768 | tf_op jit(solution)/shard_map/all_to_all | solution.py:62
  298.9 31.7 %all-to-all-start.2 = ((bf16[32,48,384]{2,1,0:T(8,128)(2,1)}), bf16[32,48,384]{2,1,0:T(8,128)(2,1)S(1)}, u32[]{:S(2)}, u32[]{:S(2)}) async-start(bf16[32,48,384]{2,1,0:T(8,128)(2,1)} %bitcast.10), calls=%async_computation.2 | async-start | bytes 2359296 | tf_op jit(solution)/shard_map/all_to_all | solution.py:61
Sparse Core Ops, SparseCore 0:
  191.3 32.0 all-gather.1
  265.1 117.8 reduce-scatter.1
where the time goes:
time: 394 us; the launch traced here: 393 us
  blocking collectives  156 us (40%)
  waiting for transfers between devices  105 us (27%)
  local copies, waits for them, and re-layouts  43.6 us (11%)
  other arithmetic  26.9 us (7%)
  starting transfers between devices  24.5 us (6%)
  matrix products  22.6 us (6%)
  between operations  14.3 us (4%)
    all_to_all x1, blocking collectives, shards(): lax.all_to_all(chosen.reshape(ep_size, slot_count, grad_out.shape[1]), 'e...  148 us
    reduce_scatter x1, waiting for transfers between devices, shards(): lax.psum_scatter(weight_term, 'dp', scatter_dimension=2, tiled=True)  47.4 us
    all_to_all x1, waiting for transfers between devices, shards(): lax.all_to_all(hid_rows, 'ep', split_axis=0, concat_axis=0, tiled=True)  27.2 us
    all_to_all x1, waiting for transfers between devices, shards(): lax.all_to_all(send_dh, 'ep', split_axis=0, concat_axis=0, tiled=True)  20 us
    another operation x2, other arithmetic  18 us
    dot_general x1, matrix products, shards(): jnp.einsum('secd,efd->secf', dy_slots, down_weight, preferred_element_typ...  11.7 us
    dot_general x1, matrix products, shards(): jnp.einsum('secf,secd->efd', scaled, dy_slots, preferred_element_type=jnp...  11 us
    gather x1, local copies, waits for them, and re-layouts, shards(): gates.reshape(pair_count)[safe_idx]  9.46 us
  transfers between devices with their start and end apart: 6, of which 5 were waited for; matrix products, arithmetic and copies ran while one was open for 11% of the time, Pallas kernels for 0%

commit v1 on v0

v1 whole, which is shorter than its diff:
```python
import jax
import jax.numpy as jnp
from jax import lax
from jax.sharding import PartitionSpec as P


def shards(grad_out, hidden, gates, expert_ids, down_weight):
    ep_size = lax.axis_size("ep")
    experts_here, hidden_part, model_width = down_weight.shape
    experts_all = ep_size * experts_here
    tok_count, top_count = expert_ids.shape
    capacity = min(tok_count, 3 * tok_count * top_count // (2 * experts_all))
    pair_count = tok_count * top_count
    slot_count = experts_here * capacity
    slots_all = experts_all * capacity
    f32, bf16 = jnp.float32, jnp.bfloat16

    expert_iota = jnp.arange(experts_all, dtype=jnp.int32)
    pair_hot = expert_ids[:, :, None] == expert_iota[None, None, :]
    tok_has = jnp.any(pair_hot, axis=1).astype(bf16)
    tok_iota = lax.optimization_barrier(jnp.arange(tok_count, dtype=jnp.int32))
    earlier = (tok_iota[None, :] < tok_iota[:, None]).astype(bf16)
    before = jnp.dot(earlier, tok_has, preferred_element_type=f32)
    rank_in = jnp.sum(jnp.where(pair_hot, before[:, None, :], 0.0), axis=2).astype(jnp.int32)
    slot_of = (expert_ids * capacity + rank_in).reshape(pair_count)

    slot_iota = lax.optimization_barrier(jnp.arange(slots_all, dtype=jnp.int32))
    sel_pair = (slot_iota[:, None] == slot_of[None, :]).astype(bf16)
    sel_tok = jnp.sum(sel_pair.reshape(slots_all, tok_count, top_count), axis=2)

    chosen = jnp.dot(sel_tok, grad_out, preferred_element_type=f32).astype(bf16)
    hid_rows = jnp.dot(
        sel_pair, hidden.reshape(pair_count, hidden_part), preferred_element_type=f32
    ).astype(bf16)
    gate_rows = jnp.dot(
        sel_pair, gates.reshape(pair_count, 1), preferred_element_type=f32
    ).astype(bf16)

    half_recv = lax.all_to_all(
        chosen.reshape(ep_size, slot_count, grad_out.shape[1]),
        "ep",
        split_axis=0,
        concat_axis=0,
        tiled=True,
    )
    hid_recv = lax.all_to_all(
        hid_rows.reshape(ep_size, slot_count, hidden_part), "ep", split_axis=0, concat_axis=0, tiled=True
    )
    gate_recv = lax.all_to_all(
        gate_rows.reshape(ep_size, slot_count), "ep", split_axis=0, concat_axis=0, tiled=True
    )
    dy_recv = lax.all_gather(half_recv, "tp", axis=2, tiled=True)
    dy_slots = dy_recv.reshape(ep_size, experts_here, capacity, model_width)
    hid_slots = hid_recv.reshape(ep_size, experts_here, capacity, hidden_part)
    gate_slots = gate_recv.reshape(ep_size, experts_here, capacity).astype(f32)

    scaled = (gate_slots[..., None] * hid_slots.astype(f32)).astype(bf16)
    weight_term = jnp.einsum("secf,secd->efd", scaled, dy_slots, preferred_element_type=f32)
    d_weight = lax.psum_scatter(
        weight_term.astype(bf16), "dp", scatter_dimension=2, tiled=True
    )

    back_proj = jnp.einsum(
        "secd,efd->secf", dy_slots, down_weight, preferred_element_type=f32
    )
    partial_value = jnp.sum(back_proj * hid_slots.astype(f32), axis=3)
    dot_total = lax.psum(partial_value, "tp")
    send_dh = (
        (gate_slots[..., None] * back_proj)
        .astype(bf16)
        .reshape(ep_size, slot_count, hidden_part)
    )
    send_dg = dot_total.astype(bf16).reshape(ep_size, slot_count)
    got_dh, got_dg = (
        lax.all_to_all(send_dh, "ep", split_axis=0, concat_axis=0, tiled=True),
        lax.all_to_all(send_dg, "ep", split_axis=0, concat_axis=0, tiled=True),
    )
    d_hidden = (
        jnp.dot(sel_pair.T, got_dh.reshape(slots_all, hidden_part), preferred_element_type=f32)
        .astype(bf16)
        .reshape(tok_count, top_count, hidden_part)
    )
    d_gates = (
        jnp.dot(sel_pair.T, got_dg.reshape(slots_all, 1), preferred_element_type=f32)
        .astype(bf16)
        .reshape(tok_count, top_count)
    )
    return (d_hidden, d_gates, d_weight)


def solution(mesh):
    placed = (
        P(("dp", "ep"), "tp"),
        P(("dp", "ep"), None, "tp"),
        P(("dp", "ep"), None),
        P(("dp", "ep"), None),
        P("ep", "tp", None),
    )
    return jax.shard_map(
        shards,
        mesh=mesh,
        in_specs=placed,
        out_specs=(P(("dp", "ep"), None, "tp"), P(("dp", "ep"), None), P("ep", "tp", "dp")),
        check_vma=False,
    )
```

time: 394 us -> 311 us (0.79)
  waiting for transfers between devices: 105 us -> 65.1 us
  local copies, waits for them, and re-layouts: 43.6 us -> 4.51 us
  other arithmetic: 26.9 us -> 10.9 us
  matrix products: 22.6 us -> 32.9 us
    reduce_scatter x1, waiting for transfers between devices: 47.4 us -> 0.01 us  [shards(): lax.psum_scatter(weight_term.astype(bf16), 'dp', scatter_dimension=2, til...]
    gather x5 -> x0, local copies, waits for them, and re-layouts: 33.1 us -> none  [the longest x1 9.46 us: shards(): gates.reshape(pair_count)[safe_idx]]
    another operation x2 -> x0, other arithmetic: 18 us -> none
    dot_general x1 -> x7, matrix products: 11 us -> 21.2 us  [the longest x1 10 us: shards(): jnp.einsum('secf,secd->efd', scaled, dy_slots, preferred_element_type=f32)]
    reduce_sum x1 -> x2, other arithmetic: 0.06 us -> 9.31 us  [the longest x1 8.56 us: shards(): sel_tok = jnp.sum(sel_pair.reshape(slots_all, tok_count, top_count), axis=2)]
    all_to_all x1, waiting for transfers between devices: 20 us -> 25.7 us  [shards(): lax.all_to_all(send_dh, 'ep', split_axis=0, concat_axis=0, tiled=True)]
    select_n x6 -> x0, other arithmetic: 4.62 us -> none  [the longest x1 3.29 us: shards(): jnp.where(filled[:, None], grad_out[safe_idx // top_count], zero_half)]
    scatter x1 -> x0, local copies, waits for them, and re-layouts: 4.32 us -> none  [shards(): source = jnp.full((experts_all * capacity,), pair_count, jnp.int32).at[sl...]
  transfers between devices with their start and end apart: 6 -> 6, of which waited for: 5 -> 4; matrix products, arithmetic and copies ran while one was open for 11% -> 8% of each run, Pallas kernels for 0% -> 0%
where the time goes in v1:
time: 311 us; the launch traced here: 307 us
  blocking collectives  157 us (50%)
  waiting for transfers between devices  65.1 us (21%)
  matrix products  32.9 us (11%)
  starting transfers between devices  22.1 us (7%)
  between operations  14.1 us (5%)
  other arithmetic  10.9 us (4%)
  local copies, waits for them, and re-layouts  4.51 us (1%)
    all_to_all x1, blocking collectives, shards(): lax.all_to_all(chosen.reshape(ep_size, slot_count, grad_out.shape[1]), 'e...  148 us
    all_to_all x1, waiting for transfers between devices, shards(): lax.all_to_all(hid_rows.reshape(ep_size, slot_count, hidden_part), 'ep',...  26.1 us
    all_to_all x1, waiting for transfers between devices, shards(): lax.all_to_all(send_dh, 'ep', split_axis=0, concat_axis=0, tiled=True)  25.7 us
    dot_general x1, matrix products, shards(): jnp.einsum('secd,efd->secf', dy_slots, down_weight, preferred_element_typ...  11.7 us
    dot_general x1, matrix products, shards(): jnp.einsum('secf,secd->efd', scaled, dy_slots, preferred_element_type=f32)  10 us
    all_to_all x1, starting transfers between devices, shards(): lax.all_to_all(gate_rows.reshape(ep_size, slot_count), 'ep', split_axis=0...  8.82 us
    psum x1, blocking collectives, shards(): dot_total = lax.psum(partial_value, 'tp')  8.79 us
    reduce_sum x1, other arithmetic, shards(): sel_tok = jnp.sum(sel_pair.reshape(slots_all, tok_count, top_count), axis=2)  8.56 us
  transfers between devices with their start and end apart: 6, of which 4 were waited for; matrix products, arithmetic and copies ran while one was open for 8% of the time, Pallas kernels for 0%

profile of v1, /device:TPU:1, one launch (start us, length us, event | category | flops | bytes accessed | tf_op | source)
XLA Modules:
  0.0 306.9 jit_solution(12810244268437048631)
XLA Ops:
  7.2 0.0 copy-start
  7.2 0.0 all-gather.2.cloned.1.call-start
  7.2 0.8 fusion.40
  8.0 0.2 fusion.41
  8.2 0.7 select_reduce_fusion
  9.0 0.7 convert_add_fusion
  9.7 8.6 %fusion.15 = bf16[1536,128]{1,0:T(8,128)(2,1)S(1)} fusion(s32[128,8]{0,1:T(8,128)S(1)} %convert_add_fusion, s32[1536]{0:T(1024)S(1)} %iota.10), kind=kLoop, calls=%fused_computation.16 | loop fusion | flops 4521984 | bytes 403456 | tf_op jit(solution)/shard_map/reduce_sum | solution.py:29
  18.2 2.8 convolution_convert_fusion
  21.1 148.4 %all_to_all.34 = bf16[32,48,2048]{2,1,0:T(8,128)(2,1)} all-to-all(bf16[32,48,2048]{2,1,0:T(8,128)(2,1)S(1)} %bitcast.39), channel_id=1, replica_groups=mesh['dp'=4,'ep'=32,'tp'=2] {'ep'}, dimensions={0} | all-to-all | bytes 12582912 | tf_op jit(solution)/shard_map/all_to_all | solution.py:39
  169.5 0.0 copy-start.1
  169.5 0.0 all-gather.2.cloned.1.call-update
  169.5 0.1 copy.70
  169.6 0.1 eq.39
  169.7 0.5 copy-done.1
  170.2 0.1 copy.71
  170.3 0.1 reshape.95
  170.4 1.1 fusion.36
  171.6 0.7 all_to_all.28
  172.3 8.8 %all-to-all-start = ((bf16[32,1,48]{2,1,0:T(2,128)(2,1)}), bf16[32,1,48]{2,1,0:T(2,128)(2,1)S(1)}, u32[]{:S(2)}, u32[]{:S(2)}) async-start(bf16[32,1,48]{2,1,0:T(2,128)(2,1)} %all_to_all.28), calls=%async_computation | async-start | bytes 32768 | tf_op jit(solution)/shard_map/all_to_all | solution.py:49
  181.1 0.0 copy-done
  181.1 2.9 fusion.24
  184.0 5.7 %all-to-all-done = bf16[32,1,48]{2,1,0:T(2,128)(2,1)S(1)} async-done(((bf16[32,1,48]{2,1,0:T(2,128)(2,1)}), bf16[32,1,48]{2,1,0:T(2,128)(2,1)S(1)}, u32[]{:S(2)}, u32[]{:S(2)}) %all-to-all-start) | async-done | bytes 3104 | tf_op jit(solution)/shard_map/all_to_all | solution.py:49
  189.7 3.9 %all-to-all-start.3 = ((bf16[32,48,384]{2,1,0:T(8,128)(2,1)}), bf16[32,48,384]{2,1,0:T(8,128)(2,1)S(1)}, u32[]{:S(2)}, u32[]{:S(2)}) async-start(bf16[32,48,384]{2,1,0:T(8,128)(2,1)} %bitcast.10), calls=%async_computation.3 | async-start | bytes 2359296 | tf_op jit(solution)/shard_map/all_to_all | solution.py:46
  193.6 0.2 reduce-scatter.2.cloned.1.call-start
  193.9 0.1 copy.73
  194.0 0.1 copy.74
  194.0 26.1 %all-to-all-done.3 = bf16[32,48,384]{2,1,0:T(8,128)(2,1)S(1)} async-done(((bf16[32,48,384]{2,1,0:T(8,128)(2,1)}), bf16[32,48,384]{2,1,0:T(8,128)(2,1)S(1)}, u32[]{:S(2)}, u32[]{:S(2)}) %all-to-all-start.3) | async-done | bytes 1179680 | tf_op jit(solution)/shard_map/all_to_all | solution.py:46
  220.1 0.0 all-gather.2.cloned.1.call-done
  220.1 10.0 %bitcast_convert_fusion = bf16[2,384,4096]{2,1,0:T(8,128)(2,1)} fusion(bf16[32,2,24,4096]{3,2,1,0:T(8,128)(2,1)} %bitcast.46, f32[32,2,24]{2,0,1:T(8,128)S(1)} %copy.74, bf16[32,2,24,384]{3,2,1,0:T(8,128)(2,1)S(1)} %bitcast.40), kind=kOutput, calls=%fused_computation | convolution fusion | flops 4836753408 | bytes 20060160 | tf_op jit(solution)/shard_map/secf,secd->efd/dot_general | solution.py:58
  230.2 0.0 reduce-scatter.2.cloned.1.call-update
  230.2 11.7 %fusion.28 = (f32[32,2,24]{2,0,1:T(8,128)S(1)}, bf16[32,2,24,384]{3,2,0,1:T(8,128)(2,1)S(1)}) fusion(f32[32,2,24]{2,0,1:T(8,128)S(1)} %copy.74, bf16[2,384,4096]{2,1,0:T(8,128)(2,1)} %param.9, bf16[32,2,24,4096]{3,2,1,0:T(8,128)(2,1)} %bitcast.47, bf16[32,2,24,384]{3,2,1,0:T(8,128)(2,1)S(1)} %bitcast.41), kind=kOutput, calls=%fused_computation.29 | convolution fusion | flops 4834785792 | bytes 21245952 | tf_op jit(solution)/shard_map/secd,efd->secf/dot_general | solution.py:63
  241.9 0.1 copy.78
  242.0 8.8 %psum.7 = bf16[32,2,24]{0,2,1:T(8,128)(2,1)S(1)} all-reduce(f32[32,2,24]{0,2,1:T(8,128)S(1)} %copy.78), channel_id=1, replica_groups=mesh['dp'=4,'ep'=32,'tp'=2] {'tp'}, use_global_device_ids=true, to_apply=%region_4.5 | all-reduce | flops 1536 | bytes 9216 | tf_op jit(solution)/shard_map/psum | solution.py:67
  250.8 0.7 copy.79
  251.5 5.1 %all-to-all-start.4 = ((bf16[32,1,48]{2,1,0:T(2,128)(2,1)}), bf16[32,1,48]{2,1,0:T(2,128)(2,1)S(1)}, u32[]{:S(2)}, u32[]{:S(2)}) async-start(bf16[32,1,48]{2,1,0:T(2,128)(2,1)} %copy.79), calls=%async_computation.4 | async-start | bytes 32768 | tf_op jit(solution)/shard_map/all_to_all | solution.py:76
  256.6 1.1 copy.76
  257.7 7.5 %all-to-all-done.4 = bf16[32,1,48]{2,1,0:T(2,128)(2,1)S(1)} async-done(((bf16[32,1,48]{2,1,0:T(2,128)(2,1)}), bf16[32,1,48]{2,1,0:T(2,128)(2,1)S(1)}, u32[]{:S(2)}, u32[]{:S(2)}) %all-to-all-start.4) | async-done | bytes 3104 | tf_op jit(solution)/shard_map/all_to_all | solution.py:76
  265.2 3.9 %all-to-all-start.2 = ((bf16[32,48,384]{2,1,0:T(8,128)(2,1)}), bf16[32,48,384]{2,1,0:T(8,128)(2,1)S(1)}, u32[]{:S(2)}, u32[]{:S(2)}) async-start(bf16[32,48,384]{2,1,0:T(8,128)(2,1)} %bitcast.6), calls=%async_computation.2 | async-start | bytes 2359296 | tf_op jit(solution)/shard_map/all_to_all | solution.py:75
  269.2 0.1 reduce.2
  269.2 0.1 reshape.98
  269.3 1.1 fusion
  270.4 0.1 reshape.92
  270.5 0.7 copy.82
  271.2 25.7 %all-to-all-done.2 = bf16[32,48,384]{2,1,0:T(8,128)(2,1)S(1)} async-done(((bf16[32,48,384]{2,1,0:T(8,128)(2,1)}), bf16[32,48,384]{2,1,0:T(8,128)(2,1)S(1)}, u32[]{:S(2)}, u32[]{:S(2)}) %all-to-all-start.2) | async-done | bytes 1179680 | tf_op jit(solution)/shard_map/all_to_all | solution.py:75
  296.9 3.1 %fusion.32 = bf16[128,8,384]{2,1,0:T(8,128)(2,1)} fusion(bf16[1536,384]{1,0:T(8,128)(2,1)S(1)} %bitcast.42, s32[1024]{0:T(1024)S(1)} %eq.39, s32[1536]{0:T(1024)S(1)} %iota.10), kind=kOutput, calls=%fused_computation.32 | convolution fusion | flops 1209925632 | bytes 1976320 | tf_op jit(solution)/shard_map/dot_general | solution.py:79
  300.0 0.0 reduce-scatter.2.cloned.1.call-done
  (3 shorter events, 0.0 us)
Async XLA Ops:
  7.2 173.9 %copy-start = (bf16[128,8,384]{2,1,0:T(8,128)(2,1)S(1)}, bf16[128,8,384]{2,1,0:T(8,128)(2,1)}, u32[]{:S(2)}) copy-start(bf16[128,8,384]{2,1,0:T(8,128)(2,1)} %param.6) | copy-start | bytes 2359300
  7.2 213.0 %all-gather.2.cloned.1.call-start = ((), (), s32[]{:S(2)}) async-start(), calls=%async_computation.6 | async-start | bytes 18874368 | tf_op jit(solution)/shard_map/all_gather | solution.py:52
  169.5 0.7 copy-start.1
  172.3 17.4 %all-to-all-start = ((bf16[32,1,48]{2,1,0:T(2,128)(2,1)}), bf16[32,1,48]{2,1,0:T(2,128)(2,1)S(1)}, u32[]{:S(2)}, u32[]{:S(2)}) async-start(bf16[32,1,48]{2,1,0:T(2,128)(2,1)} %all_to_all.28), calls=%async_computation | async-start | bytes 32768 | tf_op jit(solution)/shard_map/all_to_all | solution.py:49
  189.7 30.5 %all-to-all-start.3 = ((bf16[32,48,384]{2,1,0:T(8,128)(2,1)}), bf16[32,48,384]{2,1,0:T(8,128)(2,1)S(1)}, u32[]{:S(2)}, u32[]{:S(2)}) async-start(bf16[32,48,384]{2,1,0:T(8,128)(2,1)} %bitcast.10), calls=%async_computation.3 | async-start | bytes 2359296 | tf_op jit(solution)/shard_map/all_to_all | solution.py:46
  193.6 106.4 %reduce-scatter.2.cloned.1.call-start = ((), (), s32[]{:S(2)}) async-start(), calls=%async_computation.7 | async-start | bytes 7864320 | tf_op jit(solution)/shard_map/reduce_scatter | solution.py:59
  251.5 13.8 %all-to-all-start.4 = ((bf16[32,1,48]{2,1,0:T(2,128)(2,1)}), bf16[32,1,48]{2,1,0:T(2,128)(2,1)S(1)}, u32[]{:S(2)}, u32[]{:S(2)}) async-start(bf16[32,1,48]{2,1,0:T(2,128)(2,1)} %copy.79), calls=%async_computation.4 | async-start | bytes 32768 | tf_op jit(solution)/shard_map/all_to_all | solution.py:76
  265.2 31.7 %all-to-all-start.2 = ((bf16[32,48,384]{2,1,0:T(8,128)(2,1)}), bf16[32,48,384]{2,1,0:T(8,128)(2,1)S(1)}, u32[]{:S(2)}, u32[]{:S(2)}) async-start(bf16[32,48,384]{2,1,0:T(8,128)(2,1)} %bitcast.6), calls=%async_computation.2 | async-start | bytes 2359296 | tf_op jit(solution)/shard_map/all_to_all | solution.py:75
Sparse Core Ops, SparseCore 0:
  169.7 32.0 all-gather.1
  230.3 68.4 reduce-scatter.1

commit v2 on v1

--- a/solution.py
+++ b/solution.py
@@ -26,7 +26,9 @@
 
     slot_iota = lax.optimization_barrier(jnp.arange(slots_all, dtype=jnp.int32))
     sel_pair = (slot_iota[:, None] == slot_of[None, :]).astype(bf16)
-    sel_tok = jnp.sum(sel_pair.reshape(slots_all, tok_count, top_count), axis=2)
+    pair_iota = lax.optimization_barrier(jnp.arange(pair_count, dtype=jnp.int32))
+    tok_of_pair = (pair_iota[:, None] // top_count == tok_iota[None, :]).astype(bf16)
+    sel_tok = jnp.dot(sel_pair, tok_of_pair, preferred_element_type=f32).astype(bf16)
 
     chosen = jnp.dot(sel_tok, grad_out, preferred_element_type=f32).astype(bf16)
     hid_rows = jnp.dot(
@@ -43,12 +45,13 @@
         concat_axis=0,
         tiled=True,
     )
-    hid_recv = lax.all_to_all(
-        hid_rows.reshape(ep_size, slot_count, hidden_part), "ep", split_axis=0, concat_axis=0, tiled=True
+    flat_hid = slot_count * hidden_part
+    both = jnp.concatenate(
+        [hid_rows.reshape(ep_size, flat_hid), gate_rows.reshape(ep_size, slot_count)], axis=1
     )
-    gate_recv = lax.all_to_all(
-        gate_rows.reshape(ep_size, slot_count), "ep", split_axis=0, concat_axis=0, tiled=True
-    )
+    both_recv = lax.all_to_all(both, "ep", split_axis=0, concat_axis=0, tiled=True)
+    hid_recv = both_recv[:, :flat_hid]
+    gate_recv = both_recv[:, flat_hid:]
     dy_recv = lax.all_gather(half_recv, "tp", axis=2, tiled=True)
     dy_slots = dy_recv.reshape(ep_size, experts_here, capacity, model_width)
     hid_slots = hid_recv.reshape(ep_size, experts_here, capacity, hidden_part)
@@ -71,10 +74,10 @@
         .reshape(ep_size, slot_count, hidden_part)
     )
     send_dg = dot_total.astype(bf16).reshape(ep_size, slot_count)
-    got_dh, got_dg = (
-        lax.all_to_all(send_dh, "ep", split_axis=0, concat_axis=0, tiled=True),
-        lax.all_to_all(send_dg, "ep", split_axis=0, concat_axis=0, tiled=True),
-    )
+    back = jnp.concatenate([send_dh.reshape(ep_size, flat_hid), send_dg], axis=1)
+    got = lax.all_to_all(back, "ep", split_axis=0, concat_axis=0, tiled=True)
+    got_dh = got[:, :flat_hid]
+    got_dg = got[:, flat_hid:]
     d_hidden = (
         jnp.dot(sel_pair.T, got_dh.reshape(slots_all, hidden_part), preferred_element_type=f32)
         .astype(bf16)

time: 311 us -> 304 us (0.977); the launches traced: 307 us -> 303 us
  blocking collectives: 157 us -> 231 us
  waiting for transfers between devices: 65.1 us -> 0.04 us
  starting transfers between devices: 22.1 us -> 0.08 us
  local copies, waits for them, and re-layouts: 4.51 us -> 16.3 us
  other arithmetic: 10.9 us -> 5.71 us
  matrix products: 32.9 us -> 36.3 us
    all_to_all x0 -> x2, blocking collectives: none -> 74.1 us  [the longest x1 38.2 us: shards(): lax.all_to_all(both, 'ep', split_axis=0, concat_axis=0, tiled=True)]
    all_to_all x4 -> x0, waiting for transfers between devices: 65.1 us -> none  [the longest x1 26.1 us: shards(): lax.all_to_all(hid_rows.reshape(ep_size, slot_count, hidden_part), 'ep',...]
    all_to_all x4 -> x0, starting transfers between devices: 21.9 us -> none  [the longest x1 8.82 us: shards(): lax.all_to_all(gate_rows.reshape(ep_size, slot_count), 'ep', split_axis=0...]
    unnamed x6 -> x16, local copies, waits for them, and re-layouts: 1.25 us -> 13.5 us
    reduce_sum x1 -> x0, other arithmetic: 8.56 us -> none  [shards(): sel_tok = jnp.sum(sel_pair.reshape(slots_all, tok_count, top_count), axis=2)]
    dot_general x1, matrix products: 2.82 us -> 7.31 us  [shards(): chosen = jnp.dot(sel_tok, grad_out, preferred_element_type=f32).astype(bf16)]
    all_to_all x1 -> x4, other arithmetic: 0.06 us -> 3.31 us  [the longest x2 1.66 us: shards(): got = lax.all_to_all(back, 'ep', split_axis=0, concat_axis=0, tiled=True)]
  transfers between devices with their start and end apart: 6 -> 2, of which waited for: 4 -> 0; matrix products, arithmetic and copies ran while one was open for 8% -> 13% of each run, Pallas kernels for 0% -> 0%
where the time goes in v2:
time: 304 us; the launch traced here: 303 us
  blocking collectives  231 us (76%)
  matrix products  36.3 us (12%)
  local copies, waits for them, and re-layouts  16.3 us (5%)
  between operations  14.3 us (5%)
  other arithmetic  5.71 us (2%)
    all_to_all x1, blocking collectives, shards(): lax.all_to_all(chosen.reshape(ep_size, slot_count, grad_out.shape[1]), 'e...  149 us
    all_to_all x1, blocking collectives, shards(): lax.all_to_all(both, 'ep', split_axis=0, concat_axis=0, tiled=True)  38.2 us
    all_to_all x1, blocking collectives, shards(): got = lax.all_to_all(back, 'ep', split_axis=0, concat_axis=0, tiled=True)  36 us
    unnamed x16, local copies, waits for them, and re-layouts  13.5 us
    dot_general x1, matrix products, shards(): jnp.einsum('secd,efd->secf', dy_slots, down_weight, preferred_element_typ...  11.6 us
    dot_general x1, matrix products, shards(): jnp.einsum('secf,secd->efd', scaled, dy_slots, preferred_element_type=f32)  10 us
    psum x1, blocking collectives, shards(): dot_total = lax.psum(partial_value, 'tp')  7.9 us
    dot_general x1, matrix products, shards(): chosen = jnp.dot(sel_tok, grad_out, preferred_element_type=f32).astype(bf16)  7.31 us
  transfers between devices with their start and end apart: 2, of which 0 were waited for; matrix products, arithmetic and copies ran while one was open for 13% of the time, Pallas kernels for 0%

profile of v2, /device:TPU:1, one launch (start us, length us, event | category | flops | bytes accessed | tf_op | source)
XLA Modules:
  0.0 303.4 jit_solution(15204743121829403412)
XLA Ops:
  7.2 0.0 all-gather.2.cloned.1.call-start
  7.2 0.8 fusion.52
  8.0 0.2 fusion.55
  8.2 0.7 select_reduce_fusion
  9.0 0.7 convert_add_fusion
  9.7 0.1 copy.105
  9.8 0.1 eq.45
  9.9 7.3 %convolution_convert_fusion = bf16[1536,2048]{1,0:T(8,128)(2,1)} fusion(bf16[128,2048]{1,0:T(8,128)(2,1)} %param.5, s32[1024]{0:T(1024)S(1)} %eq.45, s32[1536]{0:T(1024)S(1)} %iota.13, s32[128]{0:T(128)S(1)} %iota.14, s32[1024]{0:T(1024)S(1)} %add_select_fusion), kind=kOutput, calls=%fused_computation.15 | convolution fusion | flops 1213005824 | bytes 6830592 | tf_op jit(solution)/shard_map/dot_general | solution.py:33
  17.2 148.6 %all_to_all.29 = bf16[32,48,2048]{2,1,0:T(8,128)(2,1)} all-to-all(bf16[32,48,2048]{2,1,0:T(8,128)(2,1)} %bitcast.48), channel_id=1, replica_groups=mesh['dp'=4,'ep'=32,'tp'=2] {'ep'}, dimensions={0} | all-to-all | bytes 12582912 | tf_op jit(solution)/shard_map/all_to_all | solution.py:41
  165.9 0.0 reduce-scatter.2.cloned.1.call-start
  165.9 1.8 fusion.27
  167.8 0.6 reshape.90
  168.4 0.1 copy-done.2
  168.5 0.1 copy.106
  168.6 0.1 reshape.102
  168.7 1.1 fusion.44
  169.8 0.1 reshape.92
  169.9 0.1 maximum_bitcast_fusion
  170.0 0.5 broadcast.23
  170.5 1.6 reduce.2
  172.1 1.2 reshape.111
  173.3 38.2 %all_to_all.30 = bf16[32,2,9240]{2,1,0:T(2,128)(2,1)} all-to-all(bf16[32,2,9240]{2,1,0:T(2,128)(2,1)S(1)} %reshape.111), channel_id=1, replica_groups=mesh['dp'=4,'ep'=32,'tp'=2] {'ep'}, dimensions={0} | all-to-all | bytes 2365440 | tf_op jit(solution)/shard_map/all_to_all | solution.py:52
  211.4 4.7 %reshape.112 = bf16[32,1,18480]{2,1,0:T(2,128)(2,1)S(1)} reshape(bf16[32,2,9240]{2,1,0:T(2,128)(2,1)} %all_to_all.30) | data formatting | bytes 2365440
  216.1 0.1 copy.139
  216.3 0.2 slice_convert_fusion
  216.4 0.4 copy.124
  216.9 0.1 copy.108
  216.9 0.1 copy.109
  217.0 10.0 %bitcast_convert_fusion = bf16[2,384,4096]{2,1,0:T(8,128)(2,1)} fusion(bf16[32,2,24,4096]{3,2,1,0:T(8,128)(2,1)} %bitcast.61, f32[32,2,24,384]{3,2,1,0:T(8,128)S(1)} %bitcast.56, f32[32,2,24]{2,0,1:T(8,128)S(1)} %copy.109), kind=kOutput, calls=%fused_computation.10 | convolution fusion | flops 4836163584 | bytes 21239808 | tf_op jit(solution)/shard_map/secf,secd->efd/dot_general | solution.py:61
  227.1 11.6 %fusion.33 = (bf16[32,2,24,384]{3,2,0,1:T(8,128)(2,1)S(1)}, f32[32,2,24]{2,0,1:T(8,128)S(1)}) fusion(f32[32,2,24]{2,0,1:T(8,128)S(1)} %copy.109, f32[32,2,24,384]{3,2,1,0:T(8,128)S(1)} %bitcast.57, bf16[2,384,4096]{2,1,0:T(8,128)(2,1)} %param.9, bf16[32,2,24,4096]{3,2,1,0:T(8,128)(2,1)} %bitcast.62), kind=kOutput, calls=%fused_computation.31 | convolution fusion | flops 4834195968 | bytes 22425600 | tf_op jit(solution)/shard_map/secd,efd->secf/dot_general | solution.py:66
  238.7 0.1 copy.111
  238.8 0.3 copy.123
  239.1 0.1 copy.113
  239.2 7.9 %psum.7 = bf16[32,2,24]{0,2,1:T(8,128)(2,1)S(1)} all-reduce(f32[32,2,24]{0,2,1:T(8,128)S(1)} %copy.113), channel_id=1, replica_groups=mesh['dp'=4,'ep'=32,'tp'=2] {'tp'}, use_global_device_ids=true, to_apply=%region_3.4 | all-reduce | flops 1536 | bytes 9216 | tf_op jit(solution)/shard_map/psum | solution.py:70
  247.1 0.1 copy.114
  247.1 0.1 maximum_bitcast_fusion.1
  247.2 1.6 reduce.3
  248.8 1.2 reshape.113
  250.0 36.0 %all_to_all.31 = bf16[32,2,9240]{2,1,0:T(2,128)(2,1)} all-to-all(bf16[32,2,9240]{2,1,0:T(2,128)(2,1)S(1)} %reshape.113), channel_id=1, replica_groups=mesh['dp'=4,'ep'=32,'tp'=2] {'ep'}, dimensions={0} | all-to-all | bytes 2365440 | tf_op jit(solution)/shard_map/all_to_all | solution.py:78
  285.9 4.7 %reshape.114 = bf16[32,1,18480]{2,1,0:T(2,128)(2,1)S(1)} reshape(bf16[32,2,9240]{2,1,0:T(2,128)(2,1)} %all_to_all.31) | data formatting | bytes 2365440
  290.6 0.1 copy.138
  290.8 0.1 slice.18
  290.9 0.6 reshape.96
  291.5 0.1 reshape.105
  291.6 1.1 fusion
  292.7 0.1 reshape.99
  292.8 0.7 copy.118
  293.4 3.1 %fusion.38 = bf16[128,8,384]{2,1,0:T(8,128)(2,1)} fusion(bf16[1536,384]{1,0:T(8,128)(2,1)S(1)} %reshape.96, s32[1024]{0:T(1024)S(1)} %eq.45, s32[1536]{0:T(1024)S(1)} %iota.13), kind=kOutput, calls=%fused_computation.35 | convolution fusion | flops 1209925632 | bytes 1976320 | tf_op jit(solution)/shard_map/dot_general | solution.py:82
  (16 shorter events, 0.1 us)
Async XLA Ops:
  7.2 158.8 %copy-start = (bf16[128,8,384]{2,1,0:T(8,128)(2,1)S(1)}, bf16[128,8,384]{2,1,0:T(8,128)(2,1)}, u32[]{:S(2)}) copy-start(bf16[128,8,384]{2,1,0:T(8,128)(2,1)} %param.6) | copy-start | bytes 2359300
  7.2 209.8 %all-gather.2.cloned.1.call-start = ((), (), s32[]{:S(2)}) async-start(), calls=%async_computation.4 | async-start | bytes 18874368 | tf_op jit(solution)/shard_map/all_gather | solution.py:55
  165.9 130.6 %reduce-scatter.2.cloned.1.call-start = ((), (), s32[]{:S(2)}) async-start(), calls=%async_computation.5 | async-start | bytes 7864320 | tf_op jit(solution)/shard_map/reduce_scatter | solution.py:62
  167.8 0.7 copy-start.2
  293.4 3.1 %copy-start.1 = (bf16[128,8,384]{2,1,0:T(8,128)(2,1)S(1)}, bf16[128,8,384]{2,1,0:T(8,128)(2,1)}, u32[]{:S(2)}) copy-start(bf16[128,8,384]{2,1,0:T(8,128)(2,1)} %param.6) | copy-start | bytes 2359300
Sparse Core Ops, SparseCore 0:
  166.0 32.0 all-gather.1
  227.2 65.8 reduce-scatter.1

commit v3 on v2

--- a/solution.py
+++ b/solution.py
@@ -26,11 +26,7 @@
 
     slot_iota = lax.optimization_barrier(jnp.arange(slots_all, dtype=jnp.int32))
     sel_pair = (slot_iota[:, None] == slot_of[None, :]).astype(bf16)
-    pair_iota = lax.optimization_barrier(jnp.arange(pair_count, dtype=jnp.int32))
-    tok_of_pair = (pair_iota[:, None] // top_count == tok_iota[None, :]).astype(bf16)
-    sel_tok = jnp.dot(sel_pair, tok_of_pair, preferred_element_type=f32).astype(bf16)
 
-    chosen = jnp.dot(sel_tok, grad_out, preferred_element_type=f32).astype(bf16)
     hid_rows = jnp.dot(
         sel_pair, hidden.reshape(pair_count, hidden_part), preferred_element_type=f32
     ).astype(bf16)
@@ -38,12 +34,21 @@
         sel_pair, gates.reshape(pair_count, 1), preferred_element_type=f32
     ).astype(bf16)
 
-    half_recv = lax.all_to_all(
-        chosen.reshape(ep_size, slot_count, grad_out.shape[1]),
-        "ep",
-        split_axis=0,
-        concat_axis=0,
-        tiled=True,
+    ids_all = lax.all_gather(expert_ids, "ep")
+    grad_all = lax.all_gather(grad_out, "ep")
+    own = lax.axis_index("ep") * experts_here + jnp.arange(experts_here, dtype=jnp.int32)
+    has_own = jnp.any(ids_all[:, :, :, None] == own[None, None, None, :], axis=2)
+    has_own_b = has_own.astype(bf16)
+    before_own = jnp.einsum("ts,bsl->btl", earlier, has_own_b, preferred_element_type=f32)
+    rank_iota = jnp.arange(capacity, dtype=jnp.int32)
+    pick = (
+        has_own[:, :, :, None]
+        & (before_own.astype(jnp.int32)[:, :, :, None] == rank_iota[None, None, None, :])
+    ).astype(bf16)
+    half_recv = (
+        jnp.einsum("btlr,btd->blrd", pick, grad_all, preferred_element_type=f32)
+        .astype(bf16)
+        .reshape(ep_size, slot_count, grad_out.shape[1])
     )
     flat_hid = slot_count * hidden_part
     both = jnp.concatenate(

time: 304 us -> 302 us (level)
  blocking collectives: 231 us -> 118 us
  waiting for transfers between devices: 0.04 us -> 106 us
  matrix products: 36.3 us -> 40 us
    all_to_all x1 -> x0, blocking collectives: 149 us -> none  [shards(): lax.all_to_all(chosen.reshape(ep_size, slot_count, grad_out.shape[1]), 'e...]
    all_gather x0 -> x1, waiting for transfers between devices: none -> 106 us  [shards(): grad_all = lax.all_gather(grad_out, 'ep')]
    all_gather x0 -> x1, blocking collectives: none -> 39.5 us  [shards(): ids_all = lax.all_gather(expert_ids, 'ep')]
    dot_general x1 -> x2, matrix products: 7.31 us -> 10.9 us  [the longest x1 10.7 us: shards(): jnp.einsum('btlr,btd->blrd', pick, grad_all, preferred_element_type=f32)]
    all_to_all x1, blocking collectives: 38.2 us -> 34.8 us  [shards(): lax.all_to_all(both, 'ep', split_axis=0, concat_axis=0, tiled=True)]
    unnamed x16 -> x20, local copies, waits for them, and re-layouts: 13.5 us -> 15 us
  transfers between devices with their start and end apart: 2 -> 3, of which waited for: 0 -> 1; matrix products, arithmetic and copies ran while one was open for 13% -> 13% of each run, Pallas kernels for 0% -> 0%
where the time goes in v3:
time: 302 us; the launch traced here: 301 us
  blocking collectives  118 us (39%)
  waiting for transfers between devices  106 us (35%)
  matrix products  40 us (13%)
  local copies, waits for them, and re-layouts  17.8 us (6%)
  between operations  14 us (5%)
  other arithmetic  5.02 us (2%)
    all_gather x1, waiting for transfers between devices, shards(): grad_all = lax.all_gather(grad_out, 'ep')  106 us
    all_gather x1, blocking collectives, shards(): ids_all = lax.all_gather(expert_ids, 'ep')  39.5 us
    all_to_all x1, blocking collectives, shards(): got = lax.all_to_all(back, 'ep', split_axis=0, concat_axis=0, tiled=True)  36 us
    all_to_all x1, blocking collectives, shards(): lax.all_to_all(both, 'ep', split_axis=0, concat_axis=0, tiled=True)  34.8 us
    unnamed x20, local copies, waits for them, and re-layouts  15 us
    dot_general x1, matrix products, shards(): jnp.einsum('secd,efd->secf', dy_slots, down_weight, preferred_element_typ...  11.6 us
    dot_general x1, matrix products, shards(): jnp.einsum('btlr,btd->blrd', pick, grad_all, preferred_element_type=f32)  10.7 us
    dot_general x1, matrix products, shards(): jnp.einsum('secf,secd->efd', scaled, dy_slots, preferred_element_type=f32)  10 us
  transfers between devices with their start and end apart: 3, of which 1 were waited for; matrix products, arithmetic and copies ran while one was open for 13% of the time, Pallas kernels for 0%

profile of v3, /device:TPU:1, one launch (start us, length us, event | category | flops | bytes accessed | tf_op | source)
XLA Modules:
  0.0 301.4 jit_solution(18253615137975418097)
XLA Ops:
  7.2 0.7 all-gather.7.cloned.1.call-update
  8.0 39.5 %all-gather = s32[4096,8]{0,1:T(8,128)S(1)} all-gather(s32[128,8]{0,1:T(8,128)} %param.8), channel_id=2, replica_groups=mesh['dp'=4,'ep'=32,'tp'=2] {'ep'}, dimensions={0}, use_global_device_ids=true | all-gather | bytes 135168 | tf_op jit(solution)/shard_map/all_gather | solution.py:37
  47.5 0.2 compare_reduce_fusion
  47.7 0.2 fusion.35
  48.0 105.6 %all-gather.7.cloned.1.call-done = bf16[4096,2048]{1,0:T(8,128)(2,1)} async-done(((bf16[128,2048]{1,0:T(8,128)(2,1)}), bf16[4096,2048]{1,0:T(8,128)(2,1)}) %all-gather.7.cloned.1.call-update) | async-done | bytes 16777232 | tf_op jit(solution)/shard_map/all_gather | solution.py:38
  153.5 10.7 %convolution_convert_fusion = bf16[32,2,24,2048]{3,2,1,0:T(8,128)(2,1)} fusion(bf16[32,128,2048,1]{2,1,3,0:T(8,128)(2,1)} %bitcast.60, s32[32,128,2]{1,2,0:T(2,128)S(1)} %copy.126, pred[32,128,2]{1,2,0:T(4,128)(4,1)S(1)} %compare_reduce_fusion), kind=kOutput, calls=%fused_computation.14 | convolution fusion | flops 808845312 | bytes 23109632 | tf_op jit(solution)/shard_map/btlr,btd->blrd/dot_general | solution.py:49
  164.3 0.6 copy-done.4
  164.9 0.1 copy.121
  165.1 0.1 reshape.92
  165.2 0.2 fusion.45
  165.5 0.1 copy.120
  165.6 0.1 eq.58
  165.7 1.1 fusion.36
  166.8 0.1 reshape.80
  166.9 1.8 fusion.23
  168.8 0.6 reshape.78
  169.4 0.1 maximum_bitcast_fusion
  169.5 0.5 broadcast.13
  170.0 1.6 reduce.2
  171.5 1.2 reshape.103
  172.7 34.8 %all_to_all.24 = bf16[32,2,9240]{2,1,0:T(2,128)(2,1)} all-to-all(bf16[32,2,9240]{2,1,0:T(2,128)(2,1)S(1)} %reshape.103), channel_id=1, replica_groups=mesh['dp'=4,'ep'=32,'tp'=2] {'ep'}, dimensions={0} | all-to-all | bytes 2365440 | tf_op jit(solution)/shard_map/all_to_all | solution.py:57
  207.5 4.7 %reshape.104 = bf16[32,1,18480]{2,1,0:T(2,128)(2,1)S(1)} reshape(bf16[32,2,9240]{2,1,0:T(2,128)(2,1)} %all_to_all.24) | data formatting | bytes 2365440
  212.2 0.1 copy.159
  212.3 1.0 copy-done.2
  213.3 0.1 copy.123
  213.4 0.1 copy.124
  213.5 1.4 slice_convert_fusion
  214.9 0.4 copy.142
  215.4 10.0 %bitcast_convert_fusion = bf16[2,384,4096]{2,1,0:T(8,128)(2,1)} fusion(bf16[32,2,24,4096]{3,2,1,0:T(8,128)(2,1)} %bitcast.74, f32[32,2,24,384]{3,2,1,0:T(8,128)S(1)} %bitcast.68, f32[32,2,24]{2,0,1:T(8,128)S(1)} %copy.124), kind=kOutput, calls=%fused_computation | convolution fusion | flops 4836163584 | bytes 21239808 | tf_op jit(solution)/shard_map/secf,secd->efd/dot_general | solution.py:66
  225.4 11.6 %fusion.26 = (bf16[32,2,24,384]{3,2,0,1:T(8,128)(2,1)S(1)}, f32[32,2,24]{2,0,1:T(8,128)S(1)}) fusion(f32[32,2,24]{2,0,1:T(8,128)S(1)} %copy.124, f32[32,2,24,384]{3,2,1,0:T(8,128)S(1)} %bitcast.69, bf16[2,384,4096]{2,1,0:T(8,128)(2,1)} %param.9, bf16[32,2,24,4096]{3,2,1,0:T(8,128)(2,1)} %bitcast.75), kind=kOutput, calls=%fused_computation.26 | convolution fusion | flops 4834195968 | bytes 22425600 | tf_op jit(solution)/shard_map/secd,efd->secf/dot_general | solution.py:71
  237.1 0.1 copy.128
  237.2 0.3 copy.141
  237.4 0.1 copy.130
  237.5 7.9 %psum.7 = bf16[32,2,24]{0,2,1:T(8,128)(2,1)S(1)} all-reduce(f32[32,2,24]{0,2,1:T(8,128)S(1)} %copy.130), channel_id=1, replica_groups=mesh['dp'=4,'ep'=32,'tp'=2] {'tp'}, use_global_device_ids=true, to_apply=%region_4.5 | all-reduce | flops 1536 | bytes 9216 | tf_op jit(solution)/shard_map/psum | solution.py:75
  245.4 0.1 copy.131
  245.5 0.1 maximum_bitcast_fusion.1
  245.6 1.6 reduce.3
  247.2 1.2 reshape.105
  248.4 36.0 %all_to_all.25 = bf16[32,2,9240]{2,1,0:T(2,128)(2,1)} all-to-all(bf16[32,2,9240]{2,1,0:T(2,128)(2,1)S(1)} %reshape.105), channel_id=1, replica_groups=mesh['dp'=4,'ep'=32,'tp'=2] {'ep'}, dimensions={0} | all-to-all | bytes 2365440 | tf_op jit(solution)/shard_map/all_to_all | solution.py:83
  284.3 4.7 %reshape.106 = bf16[32,1,18480]{2,1,0:T(2,128)(2,1)S(1)} reshape(bf16[32,2,9240]{2,1,0:T(2,128)(2,1)} %all_to_all.25) | data formatting | bytes 2365440
  289.0 0.1 copy.158
  289.2 0.1 slice.18
  289.3 0.1 reshape.97
  289.3 1.1 fusion
  290.4 0.6 reshape.84
  291.0 0.1 reshape.87
  291.1 0.7 copy.135
  291.8 3.1 %fusion.31 = bf16[128,8,384]{2,1,0:T(8,128)(2,1)} fusion(bf16[1536,384]{1,0:T(8,128)(2,1)S(1)} %reshape.84, s32[1024]{0:T(1024)S(1)} %eq.58, s32[1536]{0:T(1024)S(1)} %iota.19), kind=kOutput, calls=%fused_computation.30 | convolution fusion | flops 1209925632 | bytes 1976320 | tf_op jit(solution)/shard_map/dot_general | solution.py:87
  (25 shorter events, 0.4 us)
Async XLA Ops:
  7.2 159.8 %copy-start = (bf16[128,8,384]{2,1,0:T(8,128)(2,1)S(1)}, bf16[128,8,384]{2,1,0:T(8,128)(2,1)}, u32[]{:S(2)}) copy-start(bf16[128,8,384]{2,1,0:T(8,128)(2,1)} %param.6) | copy-start | bytes 2359300
  7.2 146.3 %all-gather.7.cloned.1.call-start = ((), (), s32[]{:S(2)}) async-start(), calls=%async_computation.5 | async-start | bytes 17301504 | tf_op jit(solution)/shard_map/all_gather | solution.py:38
  7.9 207.4 %all-gather.5.cloned.1.call-start = ((), (), s32[]{:S(2)}) async-start(), calls=%async_computation.3 | async-start | bytes 18874368 | tf_op jit(solution)/shard_map/all_gather | solution.py:60
  164.3 0.7 copy-start.4
  164.3 0.9 copy-start.3
  164.3 130.6 %reduce-scatter.2.cloned.1.call-start = ((), (), s32[]{:S(2)}) async-start(), calls=%async_computation.4 | async-start | bytes 7864320 | tf_op jit(solution)/shard_map/reduce_scatter | solution.py:67
  212.3 1.0 copy-start.2
  291.8 3.1 %copy-start.1 = (bf16[128,8,384]{2,1,0:T(8,128)(2,1)S(1)}, bf16[128,8,384]{2,1,0:T(8,128)(2,1)}, u32[]{:S(2)}) copy-start(bf16[128,8,384]{2,1,0:T(8,128)(2,1)} %param.6) | copy-start | bytes 2359300
Sparse Core Ops, SparseCore 0:
  10.6 142.8 all-gather.6
  164.4 28.5 all-gather.4
  225.5 65.6 reduce-scatter.1

commit v4 on v2

--- a/solution.py
+++ b/solution.py
@@ -26,11 +26,13 @@
 
     slot_iota = lax.optimization_barrier(jnp.arange(slots_all, dtype=jnp.int32))
     sel_pair = (slot_iota[:, None] == slot_of[None, :]).astype(bf16)
+
     pair_iota = lax.optimization_barrier(jnp.arange(pair_count, dtype=jnp.int32))
     tok_of_pair = (pair_iota[:, None] // top_count == tok_iota[None, :]).astype(bf16)
     sel_tok = jnp.dot(sel_pair, tok_of_pair, preferred_element_type=f32).astype(bf16)
-
-    chosen = jnp.dot(sel_tok, grad_out, preferred_element_type=f32).astype(bf16)
+    slot_tok = jnp.dot(
+        sel_tok, (tok_iota + 1).astype(bf16)[:, None], preferred_element_type=f32
+    ).astype(bf16)
     hid_rows = jnp.dot(
         sel_pair, hidden.reshape(pair_count, hidden_part), preferred_element_type=f32
     ).astype(bf16)
@@ -38,20 +40,31 @@
         sel_pair, gates.reshape(pair_count, 1), preferred_element_type=f32
     ).astype(bf16)
 
-    half_recv = lax.all_to_all(
-        chosen.reshape(ep_size, slot_count, grad_out.shape[1]),
-        "ep",
-        split_axis=0,
-        concat_axis=0,
-        tiled=True,
-    )
+    width = grad_out.shape[1]
+    split = width // 2
+    chosen = jnp.dot(sel_tok, grad_out[:, :split], preferred_element_type=f32).astype(bf16)
+    grad_all = lax.all_gather(grad_out[:, split:], "ep")
+
     flat_hid = slot_count * hidden_part
     both = jnp.concatenate(
-        [hid_rows.reshape(ep_size, flat_hid), gate_rows.reshape(ep_size, slot_count)], axis=1
+        [
+            hid_rows.reshape(ep_size, flat_hid),
+            gate_rows.reshape(ep_size, slot_count),
+            slot_tok.reshape(ep_size, slot_count),
+        ],
+        axis=1,
     )
     both_recv = lax.all_to_all(both, "ep", split_axis=0, concat_axis=0, tiled=True)
     hid_recv = both_recv[:, :flat_hid]
-    gate_recv = both_recv[:, flat_hid:]
+    gate_recv = both_recv[:, flat_hid : flat_hid + slot_count]
+    tok_recv = both_recv[:, flat_hid + slot_count :].astype(jnp.int32)
+
+    first_recv = lax.all_to_all(
+        chosen.reshape(ep_size, slot_count, split), "ep", split_axis=0, concat_axis=0, tiled=True
+    )
+    pick = (tok_recv[:, :, None] == (tok_iota + 1)[None, None, :]).astype(bf16)
+    rest_recv = jnp.einsum("bst,btd->bsd", pick, grad_all, preferred_element_type=f32).astype(bf16)
+    half_recv = jnp.concatenate([first_recv, rest_recv], axis=2)
     dy_recv = lax.all_gather(half_recv, "tp", axis=2, tiled=True)
     dy_slots = dy_recv.reshape(ep_size, experts_here, capacity, model_width)
     hid_slots = hid_recv.reshape(ep_size, experts_here, capacity, hidden_part)

time: 304 us -> 320 us (1.053)
  blocking collectives: 231 us -> 44.7 us
  waiting for transfers between devices: 0.04 us -> 163 us
  starting transfers between devices: 0.08 us -> 20.2 us
  local copies, waits for them, and re-layouts: 16.3 us -> 25.3 us
  other arithmetic: 5.71 us -> 11.2 us
  matrix products: 36.3 us -> 40.2 us
    all_to_all x2 -> x0, blocking collectives: 187 us -> none  [the longest x1 149 us: shards(): lax.all_to_all(chosen.reshape(ep_size, slot_count, grad_out.shape[1]), 'e...]
    all_gather x0 -> x1, waiting for transfers between devices: none -> 102 us  [shards(): grad_all = lax.all_gather(grad_out[:, split:], 'ep')]
    all_to_all x0 -> x2, waiting for transfers between devices: none -> 33.2 us  [the longest x1 33.2 us: shards(): lax.all_to_all(both, 'ep', split_axis=0, concat_axis=0, tiled=True)]
    all_gather x1, waiting for transfers between devices: 0.01 us -> 27.8 us  [shards(): dy_recv = lax.all_gather(half_recv, 'tp', axis=2, tiled=True)]
    all_to_all x0 -> x2, starting transfers between devices: none -> 19.9 us  [the longest x1 12 us: shards(): lax.all_to_all(both, 'ep', split_axis=0, concat_axis=0, tiled=True)]
    unnamed x16 -> x32, local copies, waits for them, and re-layouts: 13.5 us -> 19.5 us
    concatenate x0 -> x1, other arithmetic: none -> 5.54 us  [shards(): half_recv = jnp.concatenate([first_recv, rest_recv], axis=2)]
    all_to_all x1, blocking collectives: 36 us -> 41.3 us  [shards(): got = lax.all_to_all(back, 'ep', split_axis=0, concat_axis=0, tiled=True)]
  transfers between devices with their start and end apart: 2 -> 5, of which waited for: 0 -> 3; matrix products, arithmetic and copies ran while one was open for 13% -> 18% of each run, Pallas kernels for 0% -> 0%
where the time goes in v4:
time: 320 us; the launch traced here: 319 us
  waiting for transfers between devices  163 us (51%)
  blocking collectives  44.7 us (14%)
  matrix products  40.2 us (13%)
  local copies, waits for them, and re-layouts  25.3 us (8%)
  starting transfers between devices  20.2 us (6%)
  between operations  14 us (4%)
  other arithmetic  11.2 us (4%)
    all_gather x1, waiting for transfers between devices, shards(): grad_all = lax.all_gather(grad_out[:, split:], 'ep')  102 us
    all_to_all x1, blocking collectives, shards(): got = lax.all_to_all(back, 'ep', split_axis=0, concat_axis=0, tiled=True)  41.3 us
    all_to_all x1, waiting for transfers between devices, shards(): lax.all_to_all(both, 'ep', split_axis=0, concat_axis=0, tiled=True)  33.2 us
    all_gather x1, waiting for transfers between devices, shards(): dy_recv = lax.all_gather(half_recv, 'tp', axis=2, tiled=True)  27.8 us
    unnamed x32, local copies, waits for them, and re-layouts  19.5 us
    dot_general x1, matrix products, shards(): jnp.einsum('secd,efd->secf', dy_slots, down_weight, preferred_element_typ...  12.3 us
    all_to_all x1, starting transfers between devices, shards(): lax.all_to_all(both, 'ep', split_axis=0, concat_axis=0, tiled=True)  12 us
    dot_general x1, matrix products, shards(): jnp.einsum('secf,secd->efd', scaled, dy_slots, preferred_element_type=f32)  10 us
  transfers between devices with their start and end apart: 5, of which 3 were waited for; matrix products, arithmetic and copies ran while one was open for 18% of the time, Pallas kernels for 0%

profile of v4, /device:TPU:1, one launch (start us, length us, event | category | flops | bytes accessed | tf_op | source)
XLA Modules:
  0.0 318.7 jit_solution(6594529214081187594)
XLA Ops:
  7.2 1.7 slice.24
  9.0 0.7 fusion.52
  9.7 0.2 fusion.54
  9.9 0.7 select_reduce_fusion
  10.7 0.7 convert_add_fusion
  11.4 0.1 copy.112
  11.6 1.8 fusion.27
  13.5 0.6 reshape.100
  14.1 0.1 copy.113
  14.3 0.1 reshape.114
  14.4 1.1 fusion.42
  15.6 1.2 fusion.30
  16.8 0.2 convolution_reduce_fusion
  17.1 0.4 concatenate.9
  17.6 0.5 broadcast.38
  18.1 1.6 reduce.4
  19.7 2.0 reshape.126
  21.7 12.0 %all-to-all-start = ((bf16[32,2,9264]{2,1,0:T(2,128)(2,1)}), bf16[32,2,9264]{2,1,0:T(2,128)(2,1)}, u32[]{:S(2)}, u32[]{:S(2)}) async-start(bf16[32,2,9264]{2,1,0:T(2,128)(2,1)} %reshape.126), calls=%async_computation | async-start | bytes 2392064 | tf_op jit(solution)/shard_map/all_to_all | solution.py:57
  33.7 2.7 convolution_convert_fusion
  36.4 33.2 %all-to-all-done = bf16[32,2,9264]{2,1,0:T(2,128)(2,1)} async-done(((bf16[32,2,9264]{2,1,0:T(2,128)(2,1)}), bf16[32,2,9264]{2,1,0:T(2,128)(2,1)}, u32[]{:S(2)}, u32[]{:S(2)}) %all-to-all-start) | async-done | bytes 1185824 | tf_op jit(solution)/shard_map/all_to_all | solution.py:57
  69.6 8.0 %all-to-all-start.1 = ((bf16[32,48,1024]{2,1,0:T(8,128)(2,1)}), bf16[32,48,1024]{2,1,0:T(8,128)(2,1)S(1)}, u32[]{:S(2)}, u32[]{:S(2)}) async-start(bf16[32,48,1024]{2,1,0:T(8,128)(2,1)} %bitcast.4), calls=%async_computation.1 | async-start | bytes 6291456 | tf_op jit(solution)/shard_map/all_to_all | solution.py:62
  77.6 6.2 %reshape.127 = bf16[32,1,18528]{2,1,0:T(2,128)(2,1)} reshape(bf16[32,2,9264]{2,1,0:T(2,128)(2,1)} %all-to-all-done) | data formatting | bytes 2371584
  83.9 1.8 copy.146
  85.7 1.0 copy-done.2
  86.8 102.0 %all-gather.6.cloned.1.call-done = bf16[4096,1024]{1,0:T(8,128)(2,1)} async-done(((bf16[128,1024]{1,0:T(8,128)(2,1)}), bf16[4096,1024]{1,0:T(8,128)(2,1)}) %all-gather.6.cloned.1.call-update) | async-done | bytes 8388624 | tf_op jit(solution)/shard_map/all_gather | solution.py:46
  188.7 6.4 %convolution_convert_fusion.1 = bf16[32,48,1024]{2,1,0:T(8,128)(2,1)} fusion(bf16[32,128,1024]{2,1,0:T(8,128)(2,1)} %bitcast.54, s32[128]{0:T(128)S(1)} %broadcast_add_fusion, s32[32,48]{1,0:T(8,128)S(1)} %get-tuple-element.27), kind=kOutput, calls=%fused_computation.35 | convolution fusion | flops 404422656 | bytes 11540992 | tf_op jit(solution)/shard_map/bst,btd->bsd/dot_general | solution.py:66
  195.1 5.5 %pad_maximum_fusion = bf16[32,48,2048]{2,1,0:T(8,128)(2,1)} fusion(bf16[32,48,1024]{2,1,0:T(8,128)(2,1)} %convolution_convert_fusion.1, bf16[32,48,1024]{2,1,0:T(8,128)(2,1)S(1)} %all-to-all-done.1), kind=kLoop, calls=%fused_computation.15 | loop fusion | flops 12582912 | bytes 12582912 | tf_op jit(solution)/shard_map/concatenate | solution.py:67
  200.7 0.2 reduce-scatter.2.cloned.1.call-start
  201.1 0.9 copy-done.3
  202.0 0.2 slice_convert_fusion
  202.1 0.4 copy.131
  202.5 27.8 %all-gather.4.cloned.1.call-done = bf16[32,48,4096]{2,1,0:T(8,128)(2,1)} async-done(((bf16[32,48,2048]{2,1,0:T(8,128)(2,1)}), bf16[32,48,4096]{2,1,0:T(8,128)(2,1)}) %all-gather.4.cloned.1.call-update) | async-done | bytes 12582928 | tf_op jit(solution)/shard_map/all_gather | solution.py:68
  230.4 10.0 %bitcast_convert_fusion = bf16[2,384,4096]{2,1,0:T(8,128)(2,1)} fusion(bf16[32,2,24,4096]{3,2,1,0:T(8,128)(2,1)} %bitcast.67, f32[32,2,24,384]{3,2,1,0:T(8,128)S(1)} %bitcast.62, f32[32,2,24]{2,0,1:T(8,128)S(1)} %copy.116), kind=kOutput, calls=%fused_computation.10 | convolution fusion | flops 4836163584 | bytes 21239808 | tf_op jit(solution)/shard_map/secf,secd->efd/dot_general | solution.py:74
  240.4 12.3 %fusion.33 = (bf16[32,2,24,384]{3,2,0,1:T(8,128)(2,1)S(1)}, f32[32,2,24]{2,0,1:T(8,128)}) fusion(f32[32,2,24]{2,0,1:T(8,128)} %copy-done.5, f32[32,2,24,384]{3,2,1,0:T(8,128)S(1)} %bitcast.63, bf16[2,384,4096]{2,1,0:T(8,128)(2,1)} %param.9, bf16[32,2,24,4096]{3,2,1,0:T(8,128)(2,1)} %bitcast.68), kind=kOutput, calls=%fused_computation.32 | convolution fusion | flops 4834195968 | bytes 22425600 | tf_op jit(solution)/shard_map/secd,efd->secf/dot_general | solution.py:79
  252.7 0.8 copy.120
  253.6 3.5 %psum.7 = bf16[32,2,24]{0,2,1:T(8,128)(2,1)S(1)} all-reduce(f32[32,2,24]{0,2,1:T(8,128)S(1)} %copy.120), channel_id=1, replica_groups=mesh['dp'=4,'ep'=32,'tp'=2] {'tp'}, use_global_device_ids=true, to_apply=%region_3.4 | all-reduce | flops 1536 | bytes 9216 | tf_op jit(solution)/shard_map/psum | solution.py:83
  257.1 0.1 copy.118
  257.2 0.3 copy.130
  257.6 1.6 reduce.5
  259.2 1.2 reshape.128
  260.3 41.3 %all_to_all.29 = bf16[32,2,9240]{2,1,0:T(2,128)(2,1)} all-to-all(bf16[32,2,9240]{2,1,0:T(2,128)(2,1)S(1)} %reshape.128), channel_id=1, replica_groups=mesh['dp'=4,'ep'=32,'tp'=2] {'ep'}, dimensions={0} | all-to-all | bytes 2365440 | tf_op jit(solution)/shard_map/all_to_all | solution.py:91
  301.6 4.7 %reshape.129 = bf16[32,1,18480]{2,1,0:T(2,128)(2,1)S(1)} reshape(bf16[32,2,9240]{2,1,0:T(2,128)(2,1)} %all_to_all.29) | data formatting | bytes 2365440
  306.3 0.1 copy.145
  306.6 0.6 reshape.107
  307.3 1.1 fusion
  308.4 0.1 reshape.110
  308.5 0.7 copy.125
  309.1 3.1 fusion.38
  (44 shorter events, 1.1 us)
Async XLA Ops:
  7.2 4.4 %copy-start = (bf16[128,8,384]{2,1,0:T(8,128)(2,1)S(1)}, bf16[128,8,384]{2,1,0:T(8,128)(2,1)}, u32[]{:S(2)}) copy-start(bf16[128,8,384]{2,1,0:T(8,128)(2,1)} %param.6) | copy-start | bytes 2359300
  7.2 181.6 %all-gather.6.cloned.1.call-start = ((), (), s32[]{:S(2)}) async-start(), calls=%async_computation.6 | async-start | bytes 8650752 | tf_op jit(solution)/shard_map/all_gather | solution.py:46
  9.0 7.8 %copy-start.9 = (s32[128]{0:T(128)}, s32[128]{0:T(128)S(1)}, u32[]{:S(2)}) copy-start(s32[128]{0:T(128)S(1)} %iota.14) | copy-start | bytes 1540
  11.6 4.0 %copy-start.6 = (s32[1024]{0:T(1024)}, s32[1024]{0:T(1024)S(1)}, u32[]{:S(2)}) copy-start(s32[1024]{0:T(1024)S(1)} %eq.58) | copy-start | bytes 12292
  13.5 0.7 copy-start.8
  19.7 14.0 %copy-start.4 = (bf16[128,2048]{1,0:T(8,128)(2,1)S(1)}, bf16[128,2048]{1,0:T(8,128)(2,1)}, u32[]{:S(2)}) copy-start(bf16[128,2048]{1,0:T(8,128)(2,1)} %param.5) | copy-start | bytes 1572868
  21.7 47.9 %all-to-all-start = ((bf16[32,2,9264]{2,1,0:T(2,128)(2,1)}), bf16[32,2,9264]{2,1,0:T(2,128)(2,1)}, u32[]{:S(2)}, u32[]{:S(2)}) async-start(bf16[32,2,9264]{2,1,0:T(2,128)(2,1)} %reshape.126), calls=%async_computation | async-start | bytes 2392064 | tf_op jit(solution)/shard_map/all_to_all | solution.py:57
  69.6 8.0 %copy-start.10 = (s32[128]{0:T(128)S(1)}, s32[128]{0:T(128)}, u32[]{:S(2)}) copy-start(s32[128]{0:T(128)} %copy-done.9) | copy-start | bytes 1540
  69.6 125.6 %all-to-all-start.1 = ((bf16[32,48,1024]{2,1,0:T(8,128)(2,1)}), bf16[32,48,1024]{2,1,0:T(8,128)(2,1)S(1)}, u32[]{:S(2)}, u32[]{:S(2)}) async-start(bf16[32,48,1024]{2,1,0:T(8,128)(2,1)} %bitcast.4), calls=%async_computation.1 | async-start | bytes 6291456 | tf_op jit(solution)/shard_map/all_to_all | solution.py:62
  77.5 152.8 %all-gather.4.cloned.1.call-start = ((), (), s32[]{:S(2)}) async-start(), calls=%async_computation.4 | async-start | bytes 18874368 | tf_op jit(solution)/shard_map/all_gather | solution.py:68
  85.7 1.0 copy-start.2
  200.7 1.3 copy-start.3
  200.7 111.5 %reduce-scatter.2.cloned.1.call-start = ((), (), s32[]{:S(2)}) async-start(), calls=%async_computation.5 | async-start | bytes 7864320 | tf_op jit(solution)/shard_map/reduce_scatter | solution.py:75
  202.0 28.4 %copy-start.5 = (f32[32,2,24]{2,0,1:T(8,128)}, f32[32,2,24]{2,0,1:T(8,128)S(1)}, u32[]{:S(2)}) copy-start(f32[32,2,24]{2,0,1:T(8,128)S(1)} %copy.116) | copy-start | bytes 18436
  306.5 0.8 copy-start.7
  309.1 3.1 copy-start.1
Sparse Core Ops, SparseCore 0:
  11.2 177.5 all-gather.5
  200.8 29.4 all-gather.3
  240.5 67.0 reduce-scatter.1

commit v5 on v4

--- a/solution.py
+++ b/solution.py
@@ -40,10 +40,7 @@
         sel_pair, gates.reshape(pair_count, 1), preferred_element_type=f32
     ).astype(bf16)
 
-    width = grad_out.shape[1]
-    split = width // 2
-    chosen = jnp.dot(sel_tok, grad_out[:, :split], preferred_element_type=f32).astype(bf16)
-    grad_all = lax.all_gather(grad_out[:, split:], "ep")
+    grad_all = lax.all_gather(grad_out, "ep")
 
     flat_hid = slot_count * hidden_part
     both = jnp.concatenate(
@@ -59,12 +56,8 @@
     gate_recv = both_recv[:, flat_hid : flat_hid + slot_count]
     tok_recv = both_recv[:, flat_hid + slot_count :].astype(jnp.int32)
 
-    first_recv = lax.all_to_all(
-        chosen.reshape(ep_size, slot_count, split), "ep", split_axis=0, concat_axis=0, tiled=True
-    )
     pick = (tok_recv[:, :, None] == (tok_iota + 1)[None, None, :]).astype(bf16)
-    rest_recv = jnp.einsum("bst,btd->bsd", pick, grad_all, preferred_element_type=f32).astype(bf16)
-    half_recv = jnp.concatenate([first_recv, rest_recv], axis=2)
+    half_recv = jnp.einsum("bst,btd->bsd", pick, grad_all, preferred_element_type=f32).astype(bf16)
     dy_recv = lax.all_gather(half_recv, "tp", axis=2, tiled=True)
     dy_slots = dy_recv.reshape(ep_size, experts_here, capacity, model_width)
     hid_slots = hid_recv.reshape(ep_size, experts_here, capacity, hidden_part)

time: 320 us -> 303 us (0.947)
  starting transfers between devices: 20.2 us -> 12.3 us
  other arithmetic: 11.2 us -> 5.65 us
  local copies, waits for them, and re-layouts: 25.3 us -> 20.1 us
    all_to_all x1 -> x0, starting transfers between devices: 7.98 us -> none  [shards(): lax.all_to_all(chosen.reshape(ep_size, slot_count, split), 'ep', split_ax...]
    all_to_all x1, waiting for transfers between devices: 33.2 us -> 40.6 us  [shards(): lax.all_to_all(both, 'ep', split_axis=0, concat_axis=0, tiled=True)]
    all_gather x1, waiting for transfers between devices: 102 us -> 95.9 us  [shards(): grad_all = lax.all_gather(grad_out, 'ep')]
    concatenate x1 -> x0, other arithmetic: 5.54 us -> none  [shards(): half_recv = jnp.concatenate([first_recv, rest_recv], axis=2)]
    dot_general x1, matrix products: 6.4 us -> 10.8 us  [shards(): jnp.einsum('bst,btd->bsd', pick, grad_all, preferred_element_type=f32)]
    dot_general x2 -> x0, matrix products: 3.92 us -> none  [the longest x1 2.74 us: shards(): jnp.dot(sel_tok, grad_out[:, :split], preferred_element_type=f32)]
    unnamed x32 -> x18, local copies, waits for them, and re-layouts: 19.5 us -> 16.8 us
  transfers between devices with their start and end apart: 5 -> 4, of which waited for: 3 -> 3; matrix products, arithmetic and copies ran while one was open for 18% -> 15% of each run, Pallas kernels for 0% -> 0%
where the time goes in v5:
time: 303 us; the launch traced here: 302 us
  waiting for transfers between devices  164 us (54%)
  blocking collectives  44.8 us (15%)
  matrix products  41.1 us (14%)
  local copies, waits for them, and re-layouts  20.1 us (7%)
  between operations  14 us (5%)
  starting transfers between devices  12.3 us (4%)
  other arithmetic  5.65 us (2%)
    all_gather x1, waiting for transfers between devices, shards(): grad_all = lax.all_gather(grad_out, 'ep')  95.9 us
    all_to_all x1, blocking collectives, shards(): got = lax.all_to_all(back, 'ep', split_axis=0, concat_axis=0, tiled=True)  41.3 us
    all_to_all x1, waiting for transfers between devices, shards(): lax.all_to_all(both, 'ep', split_axis=0, concat_axis=0, tiled=True)  40.6 us
    all_gather x1, waiting for transfers between devices, shards(): dy_recv = lax.all_gather(half_recv, 'tp', axis=2, tiled=True)  26.9 us
    unnamed x18, local copies, waits for them, and re-layouts  16.8 us
    all_to_all x1, starting transfers between devices, shards(): lax.all_to_all(both, 'ep', split_axis=0, concat_axis=0, tiled=True)  12 us
    dot_general x1, matrix products, shards(): jnp.einsum('secd,efd->secf', dy_slots, down_weight, preferred_element_typ...  11.6 us
    dot_general x1, matrix products, shards(): jnp.einsum('bst,btd->bsd', pick, grad_all, preferred_element_type=f32)  10.8 us
  transfers between devices with their start and end apart: 4, of which 3 were waited for; matrix products, arithmetic and copies ran while one was open for 15% of the time, Pallas kernels for 0%

profile of v5, /device:TPU:1, one launch (start us, length us, event | category | flops | bytes accessed | tf_op | source)
XLA Modules:
  0.0 301.9 jit_solution(5631241635750547203)
XLA Ops:
  7.2 0.7 all-gather.6.cloned.1.call-update
  7.9 0.8 copy.113
  8.7 0.1 reshape.110
  8.9 0.7 fusion.59
  9.6 0.2 fusion.62
  9.8 0.7 select_reduce_fusion
  10.5 0.7 convert_add_fusion
  11.2 0.1 copy.112
  11.3 0.1 eq.58
  11.4 1.1 fusion.48
  12.6 0.1 reshape.99
  12.7 1.3 fusion.45
  13.9 0.1 reshape.100
  14.0 1.8 fusion.27
  15.9 0.6 reshape.97
  16.5 0.4 concatenate.6
  16.9 0.5 broadcast.38
  17.4 1.6 reduce.4
  19.0 2.0 reshape.122
  21.0 12.0 %all-to-all-start = ((bf16[32,2,9264]{2,1,0:T(2,128)(2,1)}), bf16[32,2,9264]{2,1,0:T(2,128)(2,1)}, u32[]{:S(2)}, u32[]{:S(2)}) async-start(bf16[32,2,9264]{2,1,0:T(2,128)(2,1)} %reshape.122), calls=%async_computation | async-start | bytes 2392064 | tf_op jit(solution)/shard_map/all_to_all | solution.py:54
  33.0 40.6 %all-to-all-done = bf16[32,2,9264]{2,1,0:T(2,128)(2,1)} async-done(((bf16[32,2,9264]{2,1,0:T(2,128)(2,1)}), bf16[32,2,9264]{2,1,0:T(2,128)(2,1)}, u32[]{:S(2)}, u32[]{:S(2)}) %all-to-all-start) | async-done | bytes 1185824 | tf_op jit(solution)/shard_map/all_to_all | solution.py:54
  73.6 4.7 %reshape.123 = bf16[32,1,18528]{2,1,0:T(2,128)(2,1)S(1)} reshape(bf16[32,2,9264]{2,1,0:T(2,128)(2,1)} %all-to-all-done) | data formatting | bytes 2371584
  78.3 0.1 copy.146
  78.5 1.0 copy-done.2
  79.5 95.9 %all-gather.6.cloned.1.call-done = bf16[4096,2048]{1,0:T(8,128)(2,1)} async-done(((bf16[128,2048]{1,0:T(8,128)(2,1)}), bf16[4096,2048]{1,0:T(8,128)(2,1)}) %all-gather.6.cloned.1.call-update) | async-done | bytes 16777232 | tf_op jit(solution)/shard_map/all_gather | solution.py:43
  175.5 10.8 %convolution_convert_fusion = bf16[32,48,2048]{2,1,0:T(8,128)(2,1)} fusion(bf16[32,128,2048]{2,1,0:T(8,128)(2,1)} %bitcast.50, s32[128]{0:T(128)S(1)} %broadcast_add_fusion, s32[32,48]{1,0:T(8,128)S(1)} %get-tuple-element.27), kind=kOutput, calls=%fused_computation.16 | convolution fusion | flops 808648704 | bytes 23075328 | tf_op jit(solution)/shard_map/bst,btd->bsd/dot_general | solution.py:60
  186.3 0.2 reduce-scatter.2.cloned.1.call-start
  186.7 0.9 copy-done.3
  187.5 0.2 slice_convert_fusion
  187.7 0.4 copy.131
  188.1 26.9 %all-gather.4.cloned.1.call-done = bf16[32,48,4096]{2,1,0:T(8,128)(2,1)} async-done(((bf16[32,48,2048]{2,1,0:T(8,128)(2,1)}), bf16[32,48,4096]{2,1,0:T(8,128)(2,1)}) %all-gather.4.cloned.1.call-update) | async-done | bytes 12582928 | tf_op jit(solution)/shard_map/all_gather | solution.py:61
  215.0 10.0 %bitcast_convert_fusion = bf16[2,384,4096]{2,1,0:T(8,128)(2,1)} fusion(bf16[32,2,24,4096]{3,2,1,0:T(8,128)(2,1)} %bitcast.64, f32[32,2,24,384]{3,2,1,0:T(8,128)S(1)} %bitcast.59, f32[32,2,24]{2,0,1:T(8,128)S(1)} %copy.116), kind=kOutput, calls=%fused_computation.10 | convolution fusion | flops 4836163584 | bytes 21239808 | tf_op jit(solution)/shard_map/secf,secd->efd/dot_general | solution.py:67
  225.1 11.6 %fusion.33 = (bf16[32,2,24,384]{3,2,0,1:T(8,128)(2,1)S(1)}, f32[32,2,24]{2,0,1:T(8,128)S(1)}) fusion(f32[32,2,24]{2,0,1:T(8,128)S(1)} %copy.116, f32[32,2,24,384]{3,2,1,0:T(8,128)S(1)} %bitcast.60, bf16[2,384,4096]{2,1,0:T(8,128)(2,1)} %param.9, bf16[32,2,24,4096]{3,2,1,0:T(8,128)(2,1)} %bitcast.65), kind=kOutput, calls=%fused_computation.31 | convolution fusion | flops 4834195968 | bytes 22425600 | tf_op jit(solution)/shard_map/secd,efd->secf/dot_general | solution.py:72
  236.7 0.1 copy.118
  236.8 0.3 copy.130
  237.2 3.5 %psum.7 = bf16[32,2,24]{0,2,1:T(8,128)(2,1)S(1)} all-reduce(f32[32,2,24]{0,2,1:T(8,128)S(1)} %copy.120), channel_id=1, replica_groups=mesh['dp'=4,'ep'=32,'tp'=2] {'tp'}, use_global_device_ids=true, to_apply=%region_3.4 | all-reduce | flops 1536 | bytes 9216 | tf_op jit(solution)/shard_map/psum | solution.py:76
  240.6 0.1 copy.121
  240.8 1.6 reduce.5
  242.4 1.2 reshape.124
  243.5 41.3 %all_to_all.24 = bf16[32,2,9240]{2,1,0:T(2,128)(2,1)} all-to-all(bf16[32,2,9240]{2,1,0:T(2,128)(2,1)S(1)} %reshape.124), channel_id=1, replica_groups=mesh['dp'=4,'ep'=32,'tp'=2] {'ep'}, dimensions={0} | all-to-all | bytes 2365440 | tf_op jit(solution)/shard_map/all_to_all | solution.py:84
  284.8 4.7 %reshape.125 = bf16[32,1,18480]{2,1,0:T(2,128)(2,1)S(1)} reshape(bf16[32,2,9240]{2,1,0:T(2,128)(2,1)} %all_to_all.24) | data formatting | bytes 2365440
  289.5 0.1 copy.145
  289.8 0.1 reshape.115
  289.9 1.1 fusion
  291.0 0.6 reshape.103
  291.5 0.1 reshape.106
  291.6 0.7 copy.125
  292.3 3.1 %fusion.38 = bf16[128,8,384]{2,1,0:T(8,128)(2,1)} fusion(bf16[1536,384]{1,0:T(8,128)(2,1)S(1)} %reshape.103, s32[1024]{0:T(1024)S(1)} %eq.58, s32[1536]{0:T(1024)S(1)} %iota.13), kind=kOutput, calls=%fused_computation.35 | convolution fusion | flops 1209925632 | bytes 1976320 | tf_op jit(solution)/shard_map/dot_general | solution.py:88
  (24 shorter events, 0.6 us)
Async XLA Ops:
  7.2 6.9 %copy-start = (bf16[128,8,384]{2,1,0:T(8,128)(2,1)S(1)}, bf16[128,8,384]{2,1,0:T(8,128)(2,1)}, u32[]{:S(2)}) copy-start(bf16[128,8,384]{2,1,0:T(8,128)(2,1)} %param.6) | copy-start | bytes 2359300
  7.2 168.3 %all-gather.6.cloned.1.call-start = ((), (), s32[]{:S(2)}) async-start(), calls=%async_computation.5 | async-start | bytes 17301504 | tf_op jit(solution)/shard_map/all_gather | solution.py:43
  21.0 52.6 %all-to-all-start = ((bf16[32,2,9264]{2,1,0:T(2,128)(2,1)}), bf16[32,2,9264]{2,1,0:T(2,128)(2,1)}, u32[]{:S(2)}, u32[]{:S(2)}) async-start(bf16[32,2,9264]{2,1,0:T(2,128)(2,1)} %reshape.122), calls=%async_computation | async-start | bytes 2392064 | tf_op jit(solution)/shard_map/all_to_all | solution.py:54
  33.0 182.0 %all-gather.4.cloned.1.call-start = ((), (), s32[]{:S(2)}) async-start(), calls=%async_computation.3 | async-start | bytes 18874368 | tf_op jit(solution)/shard_map/all_gather | solution.py:61
  78.5 1.0 copy-start.2
  186.3 1.3 copy-start.3
  186.3 109.1 %reduce-scatter.2.cloned.1.call-start = ((), (), s32[]{:S(2)}) async-start(), calls=%async_computation.4 | async-start | bytes 7864320 | tf_op jit(solution)/shard_map/reduce_scatter | solution.py:68
  292.3 3.1 %copy-start.1 = (bf16[128,8,384]{2,1,0:T(8,128)(2,1)S(1)}, bf16[128,8,384]{2,1,0:T(8,128)(2,1)}, u32[]{:S(2)}) copy-start(bf16[128,8,384]{2,1,0:T(8,128)(2,1)} %param.6) | copy-start | bytes 2359300
Sparse Core Ops, SparseCore 0:
  10.6 164.8 all-gather.5
  186.4 28.5 all-gather.3
  225.2 67.0 reduce-scatter.1

commit v6 on v2

v6 whole, which is shorter than its diff:
```python
import jax
import jax.numpy as jnp
from jax import lax
from jax.sharding import PartitionSpec as P


def shards(grad_out, hidden, gates, expert_ids, down_weight):
    ep_size = lax.axis_size("ep")
    experts_here, hidden_part, model_width = down_weight.shape
    experts_all = ep_size * experts_here
    tok_count, top_count = expert_ids.shape
    capacity = min(tok_count, 3 * tok_count * top_count // (2 * experts_all))
    pair_count = tok_count * top_count
    slot_count = experts_here * capacity
    slots_all = experts_all * capacity
    f32, bf16 = jnp.float32, jnp.bfloat16

    expert_iota = jnp.arange(experts_all, dtype=jnp.int32)
    pair_hot = expert_ids[:, :, None] == expert_iota[None, None, :]
    tok_has = jnp.any(pair_hot, axis=1).astype(bf16)
    tok_iota = lax.optimization_barrier(jnp.arange(tok_count, dtype=jnp.int32))
    earlier = (tok_iota[None, :] < tok_iota[:, None]).astype(bf16)
    before = jnp.dot(earlier, tok_has, preferred_element_type=f32)
    rank_in = jnp.sum(jnp.where(pair_hot, before[:, None, :], 0.0), axis=2).astype(jnp.int32)
    slot_of = (expert_ids * capacity + rank_in).reshape(pair_count)

    slot_iota = lax.optimization_barrier(jnp.arange(slots_all, dtype=jnp.int32))
    sel_pair = (slot_iota[:, None] == slot_of[None, :]).astype(bf16)
    pair_iota = lax.optimization_barrier(jnp.arange(pair_count, dtype=jnp.int32))
    tok_of_pair = (pair_iota[:, None] // top_count == tok_iota[None, :]).astype(bf16)
    sel_tok = jnp.dot(sel_pair, tok_of_pair, preferred_element_type=f32).astype(bf16)

    scaled_pairs = (
        gates.astype(f32)[:, :, None] * hidden.astype(f32)
    ).astype(bf16).reshape(pair_count, hidden_part)
    scaled_rows = jnp.dot(sel_pair, scaled_pairs, preferred_element_type=f32).astype(bf16)
    chosen = jnp.dot(sel_tok, grad_out, preferred_element_type=f32).astype(bf16)

    half_recv = lax.all_to_all(
        chosen.reshape(ep_size, slot_count, grad_out.shape[1]),
        "ep",
        split_axis=0,
        concat_axis=0,
        tiled=True,
    )
    scaled_recv = lax.all_to_all(
        scaled_rows.reshape(ep_size, slot_count, hidden_part), "ep", split_axis=0, concat_axis=0, tiled=True
    )
    dy_recv = lax.all_gather(half_recv, "tp", axis=2, tiled=True)
    dy_slots = dy_recv.reshape(ep_size, experts_here, capacity, model_width)
    scaled_slots = scaled_recv.reshape(ep_size, experts_here, capacity, hidden_part)

    weight_term = jnp.einsum("secf,secd->efd", scaled_slots, dy_slots, preferred_element_type=f32)
    d_weight = lax.psum_scatter(
        weight_term.astype(bf16), "dp", scatter_dimension=2, tiled=True
    )

    back_proj = jnp.einsum(
        "secd,efd->secf", dy_slots, down_weight, preferred_element_type=f32
    )
    got_bp = lax.all_to_all(
        back_proj.astype(bf16).reshape(ep_size, slot_count, hidden_part),
        "ep",
        split_axis=0,
        concat_axis=0,
        tiled=True,
    )
    bp_pairs = jnp.dot(
        sel_pair.T, got_bp.reshape(slots_all, hidden_part), preferred_element_type=f32
    ).reshape(tok_count, top_count, hidden_part)
    d_hidden = (gates.astype(f32)[:, :, None] * bp_pairs).astype(bf16)
    part_dot = jnp.sum(bp_pairs * hidden.astype(f32), axis=2)
    d_gates = lax.psum(part_dot, "tp").astype(bf16)
    return (d_hidden, d_gates, d_weight)


def solution(mesh):
    placed = (
        P(("dp", "ep"), "tp"),
        P(("dp", "ep"), None, "tp"),
        P(("dp", "ep"), None),
        P(("dp", "ep"), None),
        P("ep", "tp", None),
    )
    return jax.shard_map(
        shards,
        mesh=mesh,
        in_specs=placed,
        out_specs=(P(("dp", "ep"), None, "tp"), P(("dp", "ep"), None), P("ep", "tp", "dp")),
        check_vma=False,
    )
```

time: 304 us -> 372 us (1.22)
  waiting for transfers between devices: 0.04 us -> 117 us
  blocking collectives: 231 us -> 194 us
  local copies, waits for them, and re-layouts: 16.3 us -> 2.96 us
  starting transfers between devices: 0.08 us -> 9.35 us
    reduce_scatter x1, waiting for transfers between devices: 0.01 us -> 57.1 us  [shards(): lax.psum_scatter(weight_term.astype(bf16), 'dp', scatter_dimension=2, til...]
    all_to_all x2 -> x1, blocking collectives: 74.1 us -> 38 us  [shards(): lax.all_to_all(scaled_rows.reshape(ep_size, slot_count, hidden_part), 'ep...]
    all_gather x1, waiting for transfers between devices: 0.01 us -> 32.2 us  [shards(): dy_recv = lax.all_gather(half_recv, 'tp', axis=2, tiled=True)]
    all_to_all x0 -> x1, waiting for transfers between devices: none -> 27.2 us  [shards(): lax.all_to_all(back_proj.astype(bf16).reshape(ep_size, slot_count, hidden...]
    unnamed x16 -> x13, local copies, waits for them, and re-layouts: 13.5 us -> 1.38 us
    all_to_all x0 -> x1, starting transfers between devices: none -> 9.27 us  [shards(): lax.all_to_all(back_proj.astype(bf16).reshape(ep_size, slot_count, hidden...]
    dot_general x5 -> x3, matrix products: 17.2 us -> 14.7 us  [the longest x1 10.6 us: shards(): jnp.einsum('secf,secd->efd', scaled_slots, dy_slots, preferred_element_ty...]
  transfers between devices with their start and end apart: 2 -> 3, of which waited for: 0 -> 3; matrix products, arithmetic and copies ran while one was open for 13% -> 0% of each run, Pallas kernels for 0% -> 0%
where the time goes in v6:
time: 372 us
  blocking collectives  194 us (52%)
  waiting for transfers between devices  117 us (31%)
  matrix products  32.6 us (9%)
  between operations  14.2 us (4%)
  starting transfers between devices  9.35 us (3%)
    all_to_all x1, blocking collectives, shards(): lax.all_to_all(chosen.reshape(ep_size, slot_count, grad_out.shape[1]), 'e...  149 us
    reduce_scatter x1, waiting for transfers between devices, shards(): lax.psum_scatter(weight_term.astype(bf16), 'dp', scatter_dimension=2, til...  57.1 us
    all_to_all x1, blocking collectives, shards(): lax.all_to_all(scaled_rows.reshape(ep_size, slot_count, hidden_part), 'ep...  38 us
    all_gather x1, waiting for transfers between devices, shards(): dy_recv = lax.all_gather(half_recv, 'tp', axis=2, tiled=True)  32.2 us
    all_to_all x1, waiting for transfers between devices, shards(): lax.all_to_all(back_proj.astype(bf16).reshape(ep_size, slot_count, hidden...  27.2 us
    dot_general x1, matrix products, shards(): jnp.einsum('secd,efd->secf', dy_slots, down_weight, preferred_element_typ...  11.5 us
    dot_general x1, matrix products, shards(): jnp.einsum('secf,secd->efd', scaled_slots, dy_slots, preferred_element_ty...  10.6 us
    all_to_all x1, starting transfers between devices, shards(): lax.all_to_all(back_proj.astype(bf16).reshape(ep_size, slot_count, hidden...  9.27 us
  transfers between devices with their start and end apart: 3, of which 3 were waited for; matrix products, arithmetic and copies ran while one was open for 0% of the time, Pallas kernels for 0%

profile of v6, /device:TPU:1, one launch (start us, length us, event | category | flops | bytes accessed | tf_op | source)
XLA Modules:
  0.0 371.7 jit_solution(17722839029469389610)
XLA Ops:
  7.2 0.0 copy-start
  7.2 0.0 all-gather.2.cloned.1.call-start
  7.3 0.8 fusion.45
  8.0 0.2 fusion.48
  8.3 0.7 select_reduce_fusion
  9.0 0.7 convert_add_fusion
  9.7 0.1 copy.24
  9.8 0.1 eq.60
  9.9 0.0 copy-done
  9.9 6.2 %convolution_convert_fusion = bf16[1536,2048]{1,0:T(8,128)(2,1)} fusion(bf16[128,2048]{1,0:T(8,128)(2,1)S(1)} %copy-done, s32[1024]{0:T(1024)S(1)} %eq.60, s32[1536]{0:T(1024)S(1)} %iota.13, s32[128]{0:T(128)S(1)} %iota.14, s32[1024]{0:T(1024)S(1)} %add_select_fusion), kind=kOutput, calls=%fused_computation.9 | convolution fusion | flops 1213005824 | bytes 6830592 | tf_op jit(solution)/shard_map/dot_general | solution.py:37
  16.1 148.6 %all_to_all.15 = bf16[32,48,2048]{2,1,0:T(8,128)(2,1)} all-to-all(bf16[32,48,2048]{2,1,0:T(8,128)(2,1)} %bitcast.29), channel_id=1, replica_groups=mesh['dp'=4,'ep'=32,'tp'=2] {'ep'}, dimensions={0} | all-to-all | bytes 12582912 | tf_op jit(solution)/shard_map/all_to_all | solution.py:39
  164.8 0.0 all-gather.2.cloned.1.call-update
  164.8 32.2 %all-gather.2.cloned.1.call-done = bf16[32,48,4096]{2,1,0:T(8,128)(2,1)} async-done(((bf16[32,48,2048]{2,1,0:T(8,128)(2,1)}), bf16[32,48,4096]{2,1,0:T(8,128)(2,1)}) %all-gather.2.cloned.1.call-update) | async-done | bytes 12582928 | tf_op jit(solution)/shard_map/all_gather | solution.py:49
  197.0 11.5 %fusion.32 = bf16[32,2,24,384]{3,2,0,1:T(8,128)(2,1)S(1)} fusion(bf16[2,384,4096]{2,1,0:T(8,128)(2,1)} %param.9, bf16[32,2,24,4096]{3,2,1,0:T(8,128)(2,1)} %bitcast.33), kind=kOutput, calls=%fused_computation.27 | convolution fusion | flops 4832428032 | bytes 20054016 | tf_op jit(solution)/shard_map/secd,efd->secf/dot_general | solution.py:58
  208.5 0.0 copy-start.1
  208.5 0.0 copy-start.2
  208.5 1.1 copy.26
  209.6 9.3 %all-to-all-start.1 = ((bf16[32,48,384]{2,1,0:T(8,128)(2,1)}), bf16[32,48,384]{2,1,0:T(8,128)(2,1)S(1)}, u32[]{:S(2)}, u32[]{:S(2)}) async-start(bf16[32,48,384]{2,1,0:T(8,128)(2,1)} %bitcast.5), calls=%async_computation.1 | async-start | bytes 2359296 | tf_op jit(solution)/shard_map/all_to_all | solution.py:61
  218.9 0.0 reduce-scatter.2.cloned.1.call-start
  219.0 0.0 copy-done.1
  219.0 27.2 %all-to-all-done.1 = bf16[32,48,384]{2,1,0:T(8,128)(2,1)S(1)} async-done(((bf16[32,48,384]{2,1,0:T(8,128)(2,1)}), bf16[32,48,384]{2,1,0:T(8,128)(2,1)S(1)}, u32[]{:S(2)}, u32[]{:S(2)}) %all-to-all-start.1) | async-done | bytes 1179680 | tf_op jit(solution)/shard_map/all_to_all | solution.py:61
  246.2 0.0 copy-done.2
  246.2 0.0 slice-start
  246.2 2.3 fusion.25
  248.5 0.0 slice-start.1
  248.5 0.0 slice-start.2
  248.5 1.9 fusion.19
  250.4 38.0 %all_to_all.16 = bf16[32,48,384]{2,1,0:T(8,128)(2,1)S(1)} all-to-all(bf16[32,48,384]{2,1,0:T(8,128)(2,1)S(1)} %bitcast.31), channel_id=1, replica_groups=mesh['dp'=4,'ep'=32,'tp'=2] {'ep'}, dimensions={0} | all-to-all | bytes 2359296 | tf_op jit(solution)/shard_map/all_to_all | solution.py:46
  288.3 0.2 copy.29
  288.6 0.0 slice-done
  288.6 0.0 slice-done.1
  288.6 0.0 slice-done.2
  288.6 10.6 %bitcast_convert_fusion = bf16[2,384,4096]{2,1,0:T(8,128)(2,1)} fusion(bf16[32,2,24,384]{3,0,2,1:T(8,128)(2,1)S(1)} %bitcast.32, bf16[32,2,24,4096]{3,2,1,0:T(8,128)(2,1)S(1)} %bitcast.36), kind=kOutput, calls=%fused_computation | convolution fusion | flops 4834983936 | bytes 20054016 | tf_op jit(solution)/shard_map/secf,secd->efd/dot_general | solution.py:53
  299.2 0.0 reduce-scatter.2.cloned.1.call-update
  299.2 1.3 copy.31
  300.6 7.2 %psum.7 = bf16[128,8]{0,1:T(8,128)(2,1)} all-reduce(f32[128,8]{0,1:T(8,128)S(1)} %get-tuple-element.12), channel_id=1, replica_groups=mesh['dp'=4,'ep'=32,'tp'=2] {'tp'}, use_global_device_ids=true, to_apply=%region_3.4 | all-reduce | flops 1024 | bytes 6144 | tf_op jit(solution)/shard_map/psum | solution.py:73
  307.8 57.1 %reduce-scatter.2.cloned.1.call-done = bf16[2,384,1024]{2,1,0:T(8,128)(2,1)} async-done(((bf16[2,384,4096]{2,1,0:T(8,128)(2,1)}), bf16[2,384,1024]{2,1,0:T(8,128)(2,1)}) %reduce-scatter.2.cloned.1.call-update) | async-done | bytes 1572880 | tf_op jit(solution)/shard_map/reduce_scatter | solution.py:54
  (6 shorter events, 0.0 us)
Async XLA Ops:
  7.2 2.7 copy-start
  7.2 189.8 %all-gather.2.cloned.1.call-start = ((), (), s32[]{:S(2)}) async-start(), calls=%async_computation.4 | async-start | bytes 18874368 | tf_op jit(solution)/shard_map/all_gather | solution.py:49
  208.5 10.5 %copy-start.1 = (bf16[128,8]{0,1:T(8,128)(2,1)S(1)}, bf16[128,8]{0,1:T(8,128)(2,1)}, u32[]{:S(2)}) copy-start(bf16[128,8]{0,1:T(8,128)(2,1)} %param.7) | copy-start | bytes 6148
  208.5 37.7 %copy-start.2 = (bf16[128,8,384]{2,1,0:T(8,128)(2,1)S(1)}, bf16[128,8,384]{2,1,0:T(8,128)(2,1)}, u32[]{:S(2)}) copy-start(bf16[128,8,384]{2,1,0:T(8,128)(2,1)} %param.6) | copy-start | bytes 2359300
  209.6 36.5 %all-to-all-start.1 = ((bf16[32,48,384]{2,1,0:T(8,128)(2,1)}), bf16[32,48,384]{2,1,0:T(8,128)(2,1)S(1)}, u32[]{:S(2)}, u32[]{:S(2)}) async-start(bf16[32,48,384]{2,1,0:T(8,128)(2,1)} %bitcast.5), calls=%async_computation.1 | async-start | bytes 2359296 | tf_op jit(solution)/shard_map/all_to_all | solution.py:61
  218.9 145.9 %reduce-scatter.2.cloned.1.call-start = ((), (), s32[]{:S(2)}) async-start(), calls=%async_computation.5 | async-start | bytes 7864320 | tf_op jit(solution)/shard_map/reduce_scatter | solution.py:54
  246.2 42.4 %slice-start = ((s8[12582912]{0:T(1024)(128)(4,1)}), s8[4194304]{0:T(1024)(128)(4,1)S(1)}, s32[]{:S(2)}) async-start(s8[12582912]{0:T(1024)(128)(4,1)} %bitcast.34), calls=%async_computation.6 | async-start | bytes 8388608
  248.5 40.2 %slice-start.1 = ((s8[12582912]{0:T(1024)(128)(4,1)}), s8[4194304]{0:T(1024)(128)(4,1)S(1)}, s32[]{:S(2)}) async-start(s8[12582912]{0:T(1024)(128)(4,1)} %bitcast.34), calls=%async_computation.7 | async-start | bytes 8388608
  248.5 40.2 %slice-start.2 = ((s8[12582912]{0:T(1024)(128)(4,1)}), s8[4194304]{0:T(1024)(128)(4,1)S(1)}, s32[]{:S(2)}) async-start(s8[12582912]{0:T(1024)(128)(4,1)} %bitcast.34), calls=%async_computation.8 | async-start | bytes 8388608
Sparse Core Ops, SparseCore 0:
  164.9 32.0 all-gather.1
  299.4 65.4 reduce-scatter.1

commit v7 on v6

--- a/solution.py
+++ b/solution.py
@@ -51,12 +51,12 @@
     scaled_slots = scaled_recv.reshape(ep_size, experts_here, capacity, hidden_part)
 
     weight_term = jnp.einsum("secf,secd->efd", scaled_slots, dy_slots, preferred_element_type=f32)
-    d_weight = lax.psum_scatter(
-        weight_term.astype(bf16), "dp", scatter_dimension=2, tiled=True
-    )
+    weight_half = weight_term.astype(bf16)
+    d_weight = lax.psum_scatter(weight_half, "dp", scatter_dimension=2, tiled=True)
 
+    dy_after, _ = lax.optimization_barrier((dy_slots, weight_half))
     back_proj = jnp.einsum(
-        "secd,efd->secf", dy_slots, down_weight, preferred_element_type=f32
+        "secd,efd->secf", dy_after, down_weight, preferred_element_type=f32
     )
     got_bp = lax.all_to_all(
         back_proj.astype(bf16).reshape(ep_size, slot_count, hidden_part),

time: 372 us -> 303 us (0.81)
  waiting for transfers between devices: 117 us -> 6.86 us
  blocking collectives: 194 us -> 230 us
  local copies, waits for them, and re-layouts: 2.96 us -> 19.3 us
  starting transfers between devices: 9.35 us -> 0.08 us
    reduce_scatter x1, waiting for transfers between devices: 57.1 us -> 6.8 us  [shards(): lax.psum_scatter(weight_half, 'dp', scatter_dimension=2, tiled=True)]
    all_to_all x0 -> x1, blocking collectives: none -> 38 us  [shards(): lax.all_to_all(back_proj.astype(bf16).reshape(ep_size, slot_count, hidden...]
    all_gather x1, waiting for transfers between devices: 32.2 us -> 0.02 us  [shards(): dy_recv = lax.all_gather(half_recv, 'tp', axis=2, tiled=True)]
    all_to_all x1 -> x0, waiting for transfers between devices: 27.2 us -> none  [shards(): lax.all_to_all(back_proj.astype(bf16).reshape(ep_size, slot_count, hidden...]
    all_gather x0 -> x1, local copies, waits for them, and re-layouts: none -> 11.4 us  [shards(): dy_recv = lax.all_gather(half_recv, 'tp', axis=2, tiled=True)]
    all_to_all x1 -> x0, starting transfers between devices: 9.27 us -> none  [shards(): lax.all_to_all(back_proj.astype(bf16).reshape(ep_size, slot_count, hidden...]
    unnamed x13 -> x9, local copies, waits for them, and re-layouts: 1.38 us -> 6.98 us
  transfers between devices with their start and end apart: 3 -> 2, of which waited for: 3 -> 1; matrix products, arithmetic and copies ran while one was open for 0% -> 6% of each run, Pallas kernels for 0% -> 0%
where the time goes in v7:
time: 303 us; the launch traced here: 302 us
  blocking collectives  230 us (76%)
  matrix products  29.5 us (10%)
  local copies, waits for them, and re-layouts  19.3 us (6%)
  between operations  14.2 us (5%)
  waiting for transfers between devices  6.86 us (2%)
    all_to_all x1, blocking collectives, shards(): lax.all_to_all(chosen.reshape(ep_size, slot_count, grad_out.shape[1]), 'e...  149 us
    all_to_all x1, blocking collectives, shards(): lax.all_to_all(back_proj.astype(bf16).reshape(ep_size, slot_count, hidden...  38 us
    all_to_all x1, blocking collectives, shards(): lax.all_to_all(scaled_rows.reshape(ep_size, slot_count, hidden_part), 'ep...  37.9 us
    dot_general x1, matrix products, shards(): jnp.einsum('secd,efd->secf', dy_after, down_weight, preferred_element_typ...  11.5 us
    all_gather x1, local copies, waits for them, and re-layouts, shards(): dy_recv = lax.all_gather(half_recv, 'tp', axis=2, tiled=True)  11.4 us
    dot_general x1, matrix products, shards(): jnp.einsum('secf,secd->efd', scaled_slots, dy_slots, preferred_element_ty...  7.41 us
    unnamed x9, local copies, waits for them, and re-layouts  6.98 us
    reduce_scatter x1, waiting for transfers between devices, shards(): lax.psum_scatter(weight_half, 'dp', scatter_dimension=2, tiled=True)  6.8 us
  transfers between devices with their start and end apart: 2, of which 1 were waited for; matrix products, arithmetic and copies ran while one was open for 6% of the time, Pallas kernels for 0%

profile of v7, /device:TPU:1, one launch (start us, length us, event | category | flops | bytes accessed | tf_op | source)
XLA Modules:
  0.0 302.3 jit_solution(7368030194995690824)
XLA Ops:
  7.2 0.0 copy-start
  7.2 0.0 all-gather.2.cloned.1.call-start
  7.2 0.8 fusion.36
  8.0 0.2 fusion.39
  8.2 0.7 select_reduce_fusion
  9.0 0.7 convert_add_fusion
  9.7 0.1 copy.25
  9.8 0.1 eq.60
  9.9 0.0 copy-done
  9.9 6.3 %convolution_convert_fusion = bf16[1536,2048]{1,0:T(8,128)(2,1)} fusion(bf16[128,2048]{1,0:T(8,128)(2,1)S(1)} %copy-done, s32[1024]{0:T(1024)S(1)} %eq.60, s32[1536]{0:T(1024)S(1)} %iota.13, s32[128]{0:T(128)S(1)} %iota.14, s32[1024]{0:T(1024)S(1)} %add_select_fusion), kind=kOutput, calls=%fused_computation.5 | convolution fusion | flops 1213005824 | bytes 6830592 | tf_op jit(solution)/shard_map/dot_general | solution.py:37
  16.2 148.6 %all_to_all.15 = bf16[32,48,2048]{2,1,0:T(8,128)(2,1)} all-to-all(bf16[32,48,2048]{2,1,0:T(8,128)(2,1)} %bitcast.31), channel_id=1, replica_groups=mesh['dp'=4,'ep'=32,'tp'=2] {'ep'}, dimensions={0} | all-to-all | bytes 12582912 | tf_op jit(solution)/shard_map/all_to_all | solution.py:39
  164.8 0.0 copy-start.3
  164.8 0.0 copy-start.2
  164.8 0.0 all-gather.2.cloned.1.call-update
  164.8 0.0 reduce-scatter.2.cloned.1.call-start
  164.9 0.6 copy-done.3
  165.5 0.5 copy-done.2
  165.9 0.2 fusion.20
  166.2 1.9 fusion.14
  168.1 37.9 %all_to_all.16 = bf16[32,48,384]{2,1,0:T(8,128)(2,1)S(1)} all-to-all(bf16[32,48,384]{2,1,0:T(8,128)(2,1)S(1)} %bitcast.37), channel_id=1, replica_groups=mesh['dp'=4,'ep'=32,'tp'=2] {'ep'}, dimensions={0} | all-to-all | bytes 2359296 | tf_op jit(solution)/shard_map/all_to_all | solution.py:46
  205.9 0.2 copy.29
  206.2 0.0 all-gather.2.cloned.1.call-done
  206.2 11.4 %copy.26 = bf16[32,48,4096]{2,0,1:T(8,128)(2,1)S(1)} copy(bf16[32,48,4096]{2,1,0:T(8,128)(2,1)} %all-gather.2.cloned.1.call-done) | data formatting | bytes 25165824 | tf_op jit(solution)/shard_map/all_gather | solution.py:49
  217.6 0.0 copy-start.1
  217.6 4.6 %copy-done.1 = bf16[32,48,4096]{2,0,1:T(8,128)(2,1)} copy-done((bf16[32,48,4096]{2,0,1:T(8,128)(2,1)}, bf16[32,48,4096]{2,0,1:T(8,128)(2,1)S(1)}, u32[]{:S(2)}) %copy-start.1) | copy-done | bytes 12582936
  222.2 7.4 %bitcast_convert_fusion = bf16[2,384,4096]{2,1,0:T(8,128)(2,1)} fusion(bf16[32,2,24,384]{3,0,2,1:T(8,128)(2,1)S(1)} %bitcast.35, bf16[32,2,24,4096]{3,0,2,1:T(8,128)(2,1)S(1)} %bitcast.32), kind=kOutput, calls=%fused_computation | convolution fusion | flops 4834983936 | bytes 20054016 | tf_op jit(solution)/shard_map/secf,secd->efd/dot_general | solution.py:53
  229.6 0.0 reduce-scatter.2.cloned.1.call-update
  229.6 11.5 %fusion.25 = bf16[32,2,24,384]{3,0,2,1:T(8,128)(2,1)S(1)} fusion(bf16[32,2,24,4096]{3,0,2,1:T(8,128)(2,1)} %bitcast.33, bf16[2,384,4096]{2,1,0:T(8,128)(2,1)} %param.9), kind=kOutput, calls=%fused_computation.24 | convolution fusion | flops 4832428032 | bytes 20054016 | tf_op jit(solution)/shard_map/secd,efd->secf/dot_general | solution.py:58
  241.1 0.4 copy.30
  241.5 38.0 %all_to_all.17 = bf16[32,48,384]{2,1,0:T(8,128)(2,1)S(1)} all-to-all(bf16[32,48,384]{2,1,0:T(8,128)(2,1)S(1)} %bitcast.34), channel_id=1, replica_groups=mesh['dp'=4,'ep'=32,'tp'=2] {'ep'}, dimensions={0} | all-to-all | bytes 2359296 | tf_op jit(solution)/shard_map/all_to_all | solution.py:61
  279.5 2.2 fusion.21
  281.8 1.3 copy.31
  283.1 5.6 %psum.7 = bf16[128,8]{0,1:T(8,128)(2,1)} all-reduce(f32[128,8]{0,1:T(8,128)S(1)} %get-tuple-element.14), channel_id=1, replica_groups=mesh['dp'=4,'ep'=32,'tp'=2] {'tp'}, use_global_device_ids=true, to_apply=%region_3.4 | all-reduce | flops 1024 | bytes 6144 | tf_op jit(solution)/shard_map/psum | solution.py:73
  288.7 6.8 %reduce-scatter.2.cloned.1.call-done = bf16[2,384,1024]{2,1,0:T(8,128)(2,1)} async-done(((bf16[2,384,4096]{2,1,0:T(8,128)(2,1)}), bf16[2,384,1024]{2,1,0:T(8,128)(2,1)}) %reduce-scatter.2.cloned.1.call-update) | async-done | bytes 1572880 | tf_op jit(solution)/shard_map/reduce_scatter | solution.py:55
  (5 shorter events, 0.0 us)
Async XLA Ops:
  7.2 2.7 copy-start
  7.2 199.0 %all-gather.2.cloned.1.call-start = ((), (), s32[]{:S(2)}) async-start(), calls=%async_computation.4 | async-start | bytes 18874368 | tf_op jit(solution)/shard_map/all_gather | solution.py:49
  164.8 0.7 copy-start.3
  164.8 1.1 copy-start.2
  164.8 130.6 %reduce-scatter.2.cloned.1.call-start = ((), (), s32[]{:S(2)}) async-start(), calls=%async_computation.5 | async-start | bytes 7864320 | tf_op jit(solution)/shard_map/reduce_scatter | solution.py:55
  217.6 4.6 %copy-start.1 = (bf16[32,48,4096]{2,0,1:T(8,128)(2,1)}, bf16[32,48,4096]{2,0,1:T(8,128)(2,1)S(1)}, u32[]{:S(2)}) copy-start(bf16[32,48,4096]{2,0,1:T(8,128)(2,1)S(1)} %copy.26) | copy-start | bytes 37748740
Sparse Core Ops, SparseCore 0:
  164.9 32.0 all-gather.1
  229.8 65.6 reduce-scatter.1

commit v8 on v7

--- a/solution.py
+++ b/solution.py
@@ -54,9 +54,9 @@
     weight_half = weight_term.astype(bf16)
     d_weight = lax.psum_scatter(weight_half, "dp", scatter_dimension=2, tiled=True)
 
-    dy_after, _ = lax.optimization_barrier((dy_slots, weight_half))
+    after = (weight_half[0, 0, 0] * 0).astype(bf16)
     back_proj = jnp.einsum(
-        "secd,efd->secf", dy_after, down_weight, preferred_element_type=f32
+        "secd,efd->secf", dy_slots, down_weight + after, preferred_element_type=f32
     )
     got_bp = lax.all_to_all(
         back_proj.astype(bf16).reshape(ep_size, slot_count, hidden_part),

time: 303 us -> 302 us (level)
  no operation moved by 1% of the time
where the time goes in v8:
time: 302 us
  blocking collectives  230 us (76%)
  matrix products  29.1 us (10%)
  local copies, waits for them, and re-layouts  20.4 us (7%)
  between operations  14.8 us (5%)
  waiting for transfers between devices  5 us (2%)
    all_to_all x1, blocking collectives, shards(): lax.all_to_all(chosen.reshape(ep_size, slot_count, grad_out.shape[1]), 'e...  149 us
    all_to_all x1, blocking collectives, shards(): lax.all_to_all(back_proj.astype(bf16).reshape(ep_size, slot_count, hidden...  38 us
    all_to_all x1, blocking collectives, shards(): lax.all_to_all(scaled_rows.reshape(ep_size, slot_count, hidden_part), 'ep...  37.8 us
    dot_general x1, matrix products, shards(): jnp.einsum('secd,efd->secf', dy_slots, down_weight + after, preferred_ele...  11.5 us
    all_gather x1, local copies, waits for them, and re-layouts, shards(): dy_recv = lax.all_gather(half_recv, 'tp', axis=2, tiled=True)  11.4 us
    dot_general x1, matrix products, shards(): jnp.einsum('secf,secd->efd', scaled_slots, dy_slots, preferred_element_ty...  7.05 us
    unnamed x9, local copies, waits for them, and re-layouts  6.98 us
    dot_general x1, matrix products, shards(): chosen = jnp.dot(sel_tok, grad_out, preferred_element_type=f32).astype(bf16)  6.26 us
  transfers between devices with their start and end apart: 2, of which 1 were waited for; matrix products, arithmetic and copies ran while one was open for 6% of the time, Pallas kernels for 0%

profile of v8, /device:TPU:1, one launch (start us, length us, event | category | flops | bytes accessed | tf_op | source)
XLA Modules:
  0.0 301.9 jit_solution(9678342725313508600)
XLA Ops:
  7.2 0.0 copy-start
  7.2 0.0 all-gather.2.cloned.1.call-start
  7.2 0.8 fusion.35
  8.0 0.2 fusion.38
  8.2 0.7 select_reduce_fusion
  9.0 0.7 convert_add_fusion
  9.7 0.1 copy.33
  9.8 0.1 eq.60
  9.9 0.0 copy-done
  9.9 6.3 %convolution_convert_fusion = bf16[1536,2048]{1,0:T(8,128)(2,1)} fusion(bf16[128,2048]{1,0:T(8,128)(2,1)S(1)} %copy-done, s32[1024]{0:T(1024)S(1)} %eq.60, s32[1536]{0:T(1024)S(1)} %iota.13, s32[128]{0:T(128)S(1)} %iota.14, s32[1024]{0:T(1024)S(1)} %add_select_fusion), kind=kOutput, calls=%fused_computation.5 | convolution fusion | flops 1213005824 | bytes 6830592 | tf_op jit(solution)/shard_map/dot_general | solution.py:37
  16.2 148.7 %all_to_all.15 = bf16[32,48,2048]{2,1,0:T(8,128)(2,1)} all-to-all(bf16[32,48,2048]{2,1,0:T(8,128)(2,1)} %bitcast.30), channel_id=1, replica_groups=mesh['dp'=4,'ep'=32,'tp'=2] {'ep'}, dimensions={0} | all-to-all | bytes 12582912 | tf_op jit(solution)/shard_map/all_to_all | solution.py:39
  164.9 0.0 copy-start.3
  164.9 0.0 copy-start.2
  164.9 0.0 all-gather.2.cloned.1.call-update
  164.9 0.0 reduce-scatter.2.cloned.1.call-start
  165.0 0.6 copy-done.3
  165.6 0.5 copy-done.2
  166.0 0.2 fusion.22
  166.2 1.9 fusion.16
  168.1 37.8 %all_to_all.16 = bf16[32,48,384]{2,1,0:T(8,128)(2,1)S(1)} all-to-all(bf16[32,48,384]{2,1,0:T(8,128)(2,1)S(1)} %bitcast.35), channel_id=1, replica_groups=mesh['dp'=4,'ep'=32,'tp'=2] {'ep'}, dimensions={0} | all-to-all | bytes 2359296 | tf_op jit(solution)/shard_map/all_to_all | solution.py:46
  205.9 0.2 copy.36
  206.2 0.0 all-gather.2.cloned.1.call-done
  206.2 11.4 %copy.37 = bf16[32,48,4096]{2,0,1:T(8,128)(2,1)S(1)} copy(bf16[32,48,4096]{2,1,0:T(8,128)(2,1)} %all-gather.2.cloned.1.call-done) | data formatting | bytes 25165824 | tf_op jit(solution)/shard_map/all_gather | solution.py:49
  217.6 0.0 copy-start.1
  217.6 4.6 %copy-done.1 = bf16[32,48,4096]{2,0,1:T(8,128)(2,1)} copy-done((bf16[32,48,4096]{2,0,1:T(8,128)(2,1)}, bf16[32,48,4096]{2,0,1:T(8,128)(2,1)S(1)}, u32[]{:S(2)}) %copy-start.1) | copy-done | bytes 12582936
  222.2 7.1 %bitcast_convert_fusion = bf16[2,384,4096]{2,1,0:T(8,128)(2,1)} fusion(bf16[32,2,24,384]{3,0,2,1:T(8,128)(2,1)S(1)} %bitcast.33, bf16[32,2,24,4096]{3,0,2,1:T(8,128)(2,1)S(1)} %bitcast.31), kind=kOutput, calls=%fused_computation | convolution fusion | flops 4834983936 | bytes 20054016 | tf_op jit(solution)/shard_map/secf,secd->efd/dot_general | solution.py:53
  229.3 0.0 reduce-scatter.2.cloned.1.call-update
  229.3 1.2 slice.4
  231.1 11.5 %fusion.24 = bf16[2,384,32,24]{1,2,3,0:T(8,128)(2,1)S(1)} fusion(bf16[32,2,24,4096]{3,0,2,1:T(8,128)(2,1)} %bitcast.32, bf16[2,384,4096]{2,1,0:T(8,128)(2,1)} %param.9, bf16[]{:T(256)} %bitcast.7), kind=kOutput, calls=%fused_computation.25 | convolution fusion | flops 4845010944 | bytes 20054018 | tf_op jit(solution)/shard_map/secd,efd->secf/dot_general | solution.py:58
  242.6 0.4 copy.38
  243.0 38.0 %all_to_all.17 = bf16[32,48,384]{2,1,0:T(8,128)(2,1)S(1)} all-to-all(bf16[32,48,384]{2,1,0:T(8,128)(2,1)S(1)} %copy.38), channel_id=1, replica_groups=mesh['dp'=4,'ep'=32,'tp'=2] {'ep'}, dimensions={0} | all-to-all | bytes 2359296 | tf_op jit(solution)/shard_map/all_to_all | solution.py:61
  281.0 2.2 fusion.23
  283.2 1.3 copy.39
  284.6 5.6 %psum.7 = bf16[128,8]{0,1:T(8,128)(2,1)} all-reduce(f32[128,8]{0,1:T(8,128)S(1)} %get-tuple-element.15), channel_id=1, replica_groups=mesh['dp'=4,'ep'=32,'tp'=2] {'tp'}, use_global_device_ids=true, to_apply=%region_3.4 | all-reduce | flops 1024 | bytes 6144 | tf_op jit(solution)/shard_map/psum | solution.py:73
  290.2 4.9 %reduce-scatter.2.cloned.1.call-done = bf16[2,384,1024]{2,1,0:T(8,128)(2,1)} async-done(((bf16[2,384,4096]{2,1,0:T(8,128)(2,1)}), bf16[2,384,1024]{2,1,0:T(8,128)(2,1)}) %reduce-scatter.2.cloned.1.call-update) | async-done | bytes 1572880 | tf_op jit(solution)/shard_map/reduce_scatter | solution.py:55
  (5 shorter events, 0.0 us)
Async XLA Ops:
  7.2 2.7 copy-start
  7.2 199.0 %all-gather.2.cloned.1.call-start = ((), (), s32[]{:S(2)}) async-start(), calls=%async_computation.4 | async-start | bytes 18874368 | tf_op jit(solution)/shard_map/all_gather | solution.py:49
  164.9 0.7 copy-start.3
  164.9 1.1 copy-start.2
  164.9 130.2 %reduce-scatter.2.cloned.1.call-start = ((), (), s32[]{:S(2)}) async-start(), calls=%async_computation.5 | async-start | bytes 7864320 | tf_op jit(solution)/shard_map/reduce_scatter | solution.py:55
  217.6 4.6 %copy-start.1 = (bf16[32,48,4096]{2,0,1:T(8,128)(2,1)}, bf16[32,48,4096]{2,0,1:T(8,128)(2,1)S(1)}, u32[]{:S(2)}) copy-start(bf16[32,48,4096]{2,0,1:T(8,128)(2,1)S(1)} %copy.37) | copy-start | bytes 37748740
Sparse Core Ops, SparseCore 0:
  165.0 31.9 all-gather.1
  229.4 65.6 reduce-scatter.1

commit v9 on v3

--- a/solution.py
+++ b/solution.py
@@ -35,7 +35,6 @@
     ).astype(bf16)
 
     ids_all = lax.all_gather(expert_ids, "ep")
-    grad_all = lax.all_gather(grad_out, "ep")
     own = lax.axis_index("ep") * experts_here + jnp.arange(experts_here, dtype=jnp.int32)
     has_own = jnp.any(ids_all[:, :, :, None] == own[None, None, None, :], axis=2)
     has_own_b = has_own.astype(bf16)
@@ -45,11 +44,20 @@
         has_own[:, :, :, None]
         & (before_own.astype(jnp.int32)[:, :, :, None] == rank_iota[None, None, None, :])
     ).astype(bf16)
-    half_recv = (
-        jnp.einsum("btlr,btd->blrd", pick, grad_all, preferred_element_type=f32)
-        .astype(bf16)
-        .reshape(ep_size, slot_count, grad_out.shape[1])
-    )
+    chunk = grad_out.shape[1] // 2
+    dy_chunks = []
+    for part in range(2):
+        grad_all = lax.all_gather(grad_out[:, part * chunk : (part + 1) * chunk], "ep")
+        picked = (
+            jnp.einsum("btlr,btd->blrd", pick, grad_all, preferred_element_type=f32)
+            .astype(bf16)
+            .reshape(ep_size, slot_count, chunk)
+        )
+        dy_chunks.append(
+            lax.all_gather(picked, "tp", axis=2, tiled=True).reshape(
+                ep_size, experts_here, capacity, 2 * chunk
+            )
+        )
     flat_hid = slot_count * hidden_part
     both = jnp.concatenate(
         [hid_rows.reshape(ep_size, flat_hid), gate_rows.reshape(ep_size, slot_count)], axis=1
@@ -57,19 +65,28 @@
     both_recv = lax.all_to_all(both, "ep", split_axis=0, concat_axis=0, tiled=True)
     hid_recv = both_recv[:, :flat_hid]
     gate_recv = both_recv[:, flat_hid:]
-    dy_recv = lax.all_gather(half_recv, "tp", axis=2, tiled=True)
-    dy_slots = dy_recv.reshape(ep_size, experts_here, capacity, model_width)
     hid_slots = hid_recv.reshape(ep_size, experts_here, capacity, hidden_part)
     gate_slots = gate_recv.reshape(ep_size, experts_here, capacity).astype(f32)
 
     scaled = (gate_slots[..., None] * hid_slots.astype(f32)).astype(bf16)
-    weight_term = jnp.einsum("secf,secd->efd", scaled, dy_slots, preferred_element_type=f32)
-    d_weight = lax.psum_scatter(
-        weight_term.astype(bf16), "dp", scatter_dimension=2, tiled=True
-    )
+    w_parts = down_weight.reshape(experts_here, hidden_part, 2, 2, chunk)
+    terms = [
+        jnp.einsum("secf,secd->efd", scaled, dy_chunks[part], preferred_element_type=f32)
+        .astype(bf16)
+        .reshape(experts_here, hidden_part, 2, chunk)
+        for part in range(2)
+    ]
+    weight_half = jnp.stack(terms, axis=3).reshape(experts_here, hidden_part, model_width)
+    d_weight = lax.psum_scatter(weight_half, "dp", scatter_dimension=2, tiled=True)
 
-    back_proj = jnp.einsum(
-        "secd,efd->secf", dy_slots, down_weight, preferred_element_type=f32
+    back_proj = sum(
+        jnp.einsum(
+            "secd,efd->secf",
+            dy_chunks[part],
+            w_parts[:, :, :, part, :].reshape(experts_here, hidden_part, 2 * chunk),
+            preferred_element_type=f32,
+        )
+        for part in range(2)
     )
     partial_value = jnp.sum(back_proj * hid_slots.astype(f32), axis=3)
     dot_total = lax.psum(partial_value, "tp")

time: 302 us -> 503 us (1.67); the launches traced: 301 us -> 494 us
  local copies, waits for them, and re-layouts: 17.8 us -> 154 us
  waiting for transfers between devices: 106 us -> 135 us
  other arithmetic: 5.02 us -> 14.4 us
  blocking collectives: 118 us -> 127 us
  matrix products: 40 us -> 48.9 us
    slice x0 -> x2, local copies, waits for them, and re-layouts: none -> 77.8 us  [the longest x1 75.8 us: shards(): w_parts[:, :, :, part, :].reshape(experts_here, hidden_part, 2 * chunk)]
    another operation x1 -> x6, local copies, waits for them, and re-layouts: 0.08 us -> 33.8 us  [the longest x3 21.4 us: shards(): jnp.stack(terms, axis=3).reshape(experts_here, hidden_part, model_width)]
    all_gather x2 -> x4, waiting for transfers between devices: 106 us -> 135 us  [the longest x2 109 us: shards(): lax.all_gather(grad_out[:, part * chunk:(part + 1) * chunk], 'ep')]
    reshape x1 -> x3, local copies, waits for them, and re-layouts: 0.11 us -> 22.4 us  [the longest x1 11.1 us: shards(): jnp.stack(terms, axis=3).reshape(experts_here, hidden_part, model_width)]
    another operation x0 -> x1, other arithmetic: none -> 10.7 us  [shards(): jnp.stack(terms, axis=3).reshape(experts_here, hidden_part, model_width)]
    all_to_all x1, blocking collectives: 34.8 us -> 43.1 us  [shards(): lax.all_to_all(both, 'ep', split_axis=0, concat_axis=0, tiled=True)]
    dot_general x2 -> x4, matrix products: 21.7 us -> 28.8 us  [the longest x2 14.4 us: shards(): jnp.einsum('secf,secd->efd', scaled, dy_chunks[part], preferred_element_t...]
    all_to_all x1, blocking collectives: 36 us -> 41.3 us  [shards(): got = lax.all_to_all(back, 'ep', split_axis=0, concat_axis=0, tiled=True)]
  transfers between devices with their start and end apart: 3 -> 5, of which waited for: 1 -> 4; matrix products, arithmetic and copies ran while one was open for 13% -> 34% of each run, Pallas kernels for 0% -> 0%
where the time goes in v9:
time: 503 us; the launch traced here: 494 us
  local copies, waits for them, and re-layouts  154 us (31%)
  waiting for transfers between devices  135 us (27%)
  blocking collectives  127 us (25%)
  matrix products  48.9 us (10%)
  between operations  14.5 us (3%)
  other arithmetic  14.4 us (3%)
    all_gather x2, waiting for transfers between devices, shards(): lax.all_gather(grad_out[:, part * chunk:(part + 1) * chunk], 'ep')  109 us
    slice x1, local copies, waits for them, and re-layouts, shards(): w_parts[:, :, :, part, :].reshape(experts_here, hidden_part, 2 * chunk)  75.8 us
    all_to_all x1, blocking collectives, shards(): lax.all_to_all(both, 'ep', split_axis=0, concat_axis=0, tiled=True)  43.1 us
    all_to_all x1, blocking collectives, shards(): got = lax.all_to_all(back, 'ep', split_axis=0, concat_axis=0, tiled=True)  41.3 us
    all_gather x1, blocking collectives, shards(): ids_all = lax.all_gather(expert_ids, 'ep')  39.1 us
    all_gather x2, waiting for transfers between devices, shards(): lax.all_gather(picked, 'tp', axis=2, tiled=True)  26 us
    another operation x3, local copies, waits for them, and re-layouts, shards(): jnp.stack(terms, axis=3).reshape(experts_here, hidden_part, model_width)  21.4 us
    unnamed x24, local copies, waits for them, and re-layouts  16.1 us
  transfers between devices with their start and end apart: 5, of which 4 were waited for; matrix products, arithmetic and copies ran while one was open for 34% of the time, Pallas kernels for 0%

profile of v9, /device:TPU:1, one launch (start us, length us, event | category | flops | bytes accessed | tf_op | source)
XLA Modules:
  0.0 494.5 jit_solution(8450872517063432246)
XLA Ops:
  7.2 1.9 fusion.66
  9.2 0.7 all-gather.12.cloned.1.call-update
  10.0 39.1 %all-gather = s32[4096,8]{0,1:T(8,128)S(1)} all-gather(s32[128,8]{0,1:T(8,128)} %param.8), channel_id=2, replica_groups=mesh['dp'=4,'ep'=32,'tp'=2] {'ep'}, dimensions={0}, use_global_device_ids=true | all-gather | bytes 135168 | tf_op jit(solution)/shard_map/all_gather | solution.py:37
  49.3 0.2 fusion.46
  49.5 62.5 %all-gather.14.cloned.1.call-done = bf16[4096,1024]{1,0:T(8,128)(2,1)} async-done(((bf16[128,1024]{1,0:T(8,128)(2,1)}), bf16[4096,1024]{1,0:T(8,128)(2,1)}) %all-gather.14.cloned.1.call-update) | async-done | bytes 8388624 | tf_op jit(solution)/shard_map/all_gather | solution.py:50
  112.1 6.3 %convolution_convert_fusion = bf16[32,2,24,1024]{3,2,1,0:T(8,128)(2,1)} fusion(bf16[32,128,1024,1]{2,1,3,0:T(8,128)(2,1)} %bitcast.74, s32[32,128,2]{1,2,0:T(2,128)S(1)} %copy.166, pred[32,128,2]{1,2,0:T(4,128)(4,1)S(1)} %compare_reduce_fusion), kind=kOutput, calls=%fused_computation.37 | convolution fusion | flops 404619264 | bytes 11575296 | tf_op jit(solution)/shard_map/btlr,btd->blrd/dot_general | solution.py:52
  118.4 0.6 copy-done.5
  119.3 0.2 fusion.59
  119.8 1.1 fusion.47
  121.0 1.8 fusion.30
  122.9 0.6 reshape.90
  123.6 0.5 broadcast.15
  124.1 1.6 reduce.6
  125.7 1.2 reshape.128
  126.8 43.1 %all_to_all.24 = bf16[32,2,9240]{2,1,0:T(2,128)(2,1)} all-to-all(bf16[32,2,9240]{2,1,0:T(2,128)(2,1)S(1)} %reshape.128), channel_id=1, replica_groups=mesh['dp'=4,'ep'=32,'tp'=2] {'ep'}, dimensions={0} | all-to-all | bytes 2365440 | tf_op jit(solution)/shard_map/all_to_all | solution.py:65
  169.9 4.7 reshape.129
  174.8 1.0 copy-done.2
  175.9 46.1 %all-gather.12.cloned.1.call-done = bf16[4096,1024]{1,0:T(8,128)(2,1)} async-done(((bf16[128,1024]{1,0:T(8,128)(2,1)}), bf16[4096,1024]{1,0:T(8,128)(2,1)}) %all-gather.12.cloned.1.call-update) | async-done | bytes 8388624 | tf_op jit(solution)/shard_map/all_gather | solution.py:50
  222.0 6.3 %convolution_convert_fusion.1 = bf16[32,2,24,1024]{3,2,1,0:T(8,128)(2,1)} fusion(bf16[32,128,1024,1]{2,1,3,0:T(8,128)(2,1)} %bitcast.73, s32[32,128,2]{1,2,0:T(2,128)S(1)} %copy.166, pred[32,128,2]{1,2,0:T(4,128)(4,1)S(1)} %compare_reduce_fusion), kind=kOutput, calls=%fused_computation.38 | convolution fusion | flops 404619264 | bytes 11575296 | tf_op jit(solution)/shard_map/btlr,btd->blrd/dot_general | solution.py:52
  228.4 0.2 reduce-scatter.2.cloned.1.call-start
  228.6 1.0 copy-done.3
  229.8 0.4 copy.192
  230.2 14.3 %all-gather.10.cloned.1.call-done = bf16[32,48,2048]{2,1,0:T(8,128)(2,1)} async-done(((bf16[32,48,1024]{2,1,0:T(8,128)(2,1)}), bf16[32,48,2048]{2,1,0:T(8,128)(2,1)}) %all-gather.10.cloned.1.call-update) | async-done | bytes 6291472 | tf_op jit(solution)/shard_map/all_gather | solution.py:57
  244.5 7.2 %bitcast_convert_fusion = bf16[2,384,2048]{2,1,0:T(8,128)(2,1)} fusion(bf16[32,2,24,2048]{3,2,1,0:T(8,128)(2,1)} %bitcast.91, f32[32,2,24,384]{3,2,1,0:T(8,128)S(1)} %bitcast.84, f32[32,2,24]{2,0,1:T(8,128)S(1)} %copy.164), kind=kOutput, calls=%fused_computation.11 | convolution fusion | flops 2418671616 | bytes 11802624 | tf_op jit(solution)/shard_map/secf,secd->efd/dot_general | solution.py:74
  251.7 6.2 %stack_reshape.7 = bf16[2,384,2,1,1024]{4,2,1,0,3:T(2,128)(2,1)} reshape(bf16[2,384,2048]{2,1,0:T(8,128)(2,1)} %bitcast_convert_fusion) | data formatting | bytes 6291456 | tf_op jit(solution)/shard_map/stack;reshape | solution.py:79
  257.9 11.7 %all-gather.8.cloned.1.call-done = bf16[32,48,2048]{2,1,0:T(8,128)(2,1)} async-done(((bf16[32,48,1024]{2,1,0:T(8,128)(2,1)}), bf16[32,48,2048]{2,1,0:T(8,128)(2,1)}) %all-gather.8.cloned.1.call-update) | async-done | bytes 6291472 | tf_op jit(solution)/shard_map/all_gather | solution.py:57
  269.6 7.2 %bitcast_convert_fusion.1 = bf16[2,384,2048]{2,1,0:T(8,128)(2,1)} fusion(bf16[32,2,24,2048]{3,2,1,0:T(8,128)(2,1)} %bitcast.93, f32[32,2,24,384]{3,2,1,0:T(8,128)S(1)} %bitcast.85, f32[32,2,24]{2,0,1:T(8,128)S(1)} %copy.164), kind=kOutput, calls=%fused_computation.12 | convolution fusion | flops 2418671616 | bytes 11802624 | tf_op jit(solution)/shard_map/secf,secd->efd/dot_general | solution.py:74
  276.8 6.2 %stack_reshape.6 = bf16[2,384,2,1,1024]{4,2,1,0,3:T(2,128)(2,1)} reshape(bf16[2,384,2048]{2,1,0:T(8,128)(2,1)} %bitcast_convert_fusion.1) | data formatting | bytes 6291456 | tf_op jit(solution)/shard_map/stack;reshape | solution.py:79
  283.0 10.7 %pad_maximum_fusion = bf16[2,384,2,2,1024]{4,2,1,0,3:T(2,128)(2,1)S(1)} fusion(bf16[2,384,2,1,1024]{4,2,1,0,3:T(2,128)(2,1)} %stack_reshape.7, bf16[2,384,2,1,1024]{4,2,1,0,3:T(2,128)(2,1)} %stack_reshape.6), kind=kLoop, calls=%fused_computation.10 | loop fusion | flops 3145728 | bytes 12582912 | tf_op jit(solution)/shard_map/stack | solution.py:79
  293.7 9.1 %copy.179 = bf16[2,384,2,2,1024]{4,3,2,1,0:T(2,128)(2,1)} copy(bf16[2,384,2,2,1024]{4,2,1,0,3:T(2,128)(2,1)S(1)} %pad_maximum_fusion) | data formatting | bytes 12582912 | tf_op jit(solution)/shard_map/stack | solution.py:79
  302.8 11.1 %reshape.103 = bf16[2,384,4096]{2,1,0:T(8,128)(2,1)} reshape(bf16[2,384,2,2,1024]{4,3,2,1,0:T(2,128)(2,1)} %copy.179) | data formatting | bytes 12582912 | tf_op jit(solution)/shard_map/reshape | solution.py:79
  313.9 11.1 %reshape.95 = bf16[2,384,2,2,1024]{4,3,2,1,0:T(2,128)(2,1)} reshape(bf16[2,384,4096]{2,1,0:T(8,128)(2,1)} %param.9) | data formatting | bytes 12582912 | tf_op jit(solution)/shard_map/reshape | solution.py:72
  325.0 75.8 %slice_reduce_fusion.1 = (bf16[2,384,2,1024]{3,2,1,0:T(2,128)(2,1)}, bf16[2,384,2,1024]{3,2,1,0:T(2,128)(2,1)}) fusion(bf16[2,384,2,2,1024]{4,3,2,1,0:T(2,128)(2,1)} %reshape.95), kind=kLoop, calls=%fused_computation.9 | loop fusion | bytes 12582912 | tf_op jit(solution)/shard_map/slice | solution.py:86
  400.9 6.2 %reshape.115 = bf16[2,384,2048,1]{2,1,0,3:T(8,128)(2,1)} reshape(bf16[2,384,2,1024]{3,2,1,0:T(2,128)(2,1)} %get-tuple-element.25) | data formatting | bytes 6291456 | tf_op jit(solution)/shard_map/reshape;squeeze | solution.py:86
  407.0 6.1 %reshape.113 = bf16[2,384,2048,1]{2,1,0,3:T(8,128)(2,1)} reshape(bf16[2,384,2,1024]{3,2,1,0:T(2,128)(2,1)} %get-tuple-element.24) | data formatting | bytes 6291456 | tf_op jit(solution)/shard_map/reshape;squeeze | solution.py:86
  413.2 6.9 %fusion.10 = f32[2,32,24,384]{3,2,1,0:T(8,128)S(1)} fusion(bf16[32,2,24,2048]{3,2,1,0:T(8,128)(2,1)} %bitcast.92, bf16[2,384,2048,1]{2,1,0,3:T(8,128)(2,1)} %reshape.115), kind=kOutput, calls=%fused_computation.15 | convolution fusion | flops 2415919104 | bytes 11796480 | tf_op jit(solution)/shard_map/secd,efd->secf/dot_general | solution.py:83
  420.0 7.5 %fusion.33 = (bf16[32,2,24,384]{3,2,0,1:T(8,128)(2,1)}, f32[32,2,24]{2,0,1:T(8,128)S(1)}) fusion(f32[32,2,24]{2,0,1:T(8,128)S(1)} %copy.164, f32[32,2,24,384]{3,2,1,0:T(8,128)S(1)} %bitcast.86, f32[2,32,24,384]{3,2,1,0:T(8,128)S(1)} %fusion.10, bf16[2,384,2048,1]{2,1,0,3:T(8,128)(2,1)S(1)} %copy-done.4, bf16[32,2,24,2048]{3,2,1,0:T(8,128)(2,1)} %bitcast.94), kind=kOutput, calls=%fused_computation.34 | convolution fusion | flops 2418866688 | bytes 15347712 | tf_op jit(solution)/shard_map/secd,efd->secf/dot_general | solution.py:83
  427.6 3.5 psum.7
  431.2 1.4 copy.171
  432.6 0.3 copy.191
  432.9 1.6 reduce.7
  434.5 1.2 reshape.130
  435.6 41.3 %all_to_all.25 = bf16[32,2,9240]{2,1,0:T(2,128)(2,1)} all-to-all(bf16[32,2,9240]{2,1,0:T(2,128)(2,1)S(1)} %reshape.130), channel_id=1, replica_groups=mesh['dp'=4,'ep'=32,'tp'=2] {'ep'}, dimensions={0} | all-to-all | bytes 2365440 | tf_op jit(solution)/shard_map/all_to_all | solution.py:100
  476.9 4.7 reshape.131
  481.9 0.6 reshape.99
  482.5 1.1 fusion
  483.7 0.7 copy.180
  484.4 3.1 fusion.43
  (48 shorter events, 2.2 us)
Async XLA Ops:
  7.2 113.9 %copy-start = (bf16[128,8,384]{2,1,0:T(8,128)(2,1)S(1)}, bf16[128,8,384]{2,1,0:T(8,128)(2,1)}, u32[]{:S(2)}) copy-start(bf16[128,8,384]{2,1,0:T(8,128)(2,1)} %param.6) | copy-start | bytes 2359300
  7.2 104.9 %all-gather.14.cloned.1.call-start = ((), (), s32[]{:S(2)}) async-start(), calls=%async_computation.7 | async-start | bytes 8650752 | tf_op jit(solution)/shard_map/all_gather | solution.py:50
  9.2 212.9 %all-gather.12.cloned.1.call-start = ((), (), s32[]{:S(2)}) async-start(), calls=%async_computation.6 | async-start | bytes 8650752 | tf_op jit(solution)/shard_map/all_gather | solution.py:50
  9.9 234.6 %all-gather.10.cloned.1.call-start = ((), (), s32[]{:S(2)}) async-start(), calls=%async_computation.4 | async-start | bytes 9437184 | tf_op jit(solution)/shard_map/all_gather | solution.py:57
  118.4 0.7 copy-start.5
  118.4 0.7 copy-start.6
  118.4 151.2 %all-gather.8.cloned.1.call-start = ((), (), s32[]{:S(2)}) async-start(), calls=%async_computation.3 | async-start | bytes 9437184 | tf_op jit(solution)/shard_map/all_gather | solution.py:57
  174.8 1.0 copy-start.2
  228.3 1.3 copy-start.3
  228.4 259.1 %reduce-scatter.2.cloned.1.call-start = ((), (), s32[]{:S(2)}) async-start(), calls=%async_computation.5 | async-start | bytes 7864320 | tf_op jit(solution)/shard_map/reduce_scatter | solution.py:80
  413.2 6.9 %copy-start.4 = (bf16[2,384,2048,1]{2,1,0,3:T(8,128)(2,1)S(1)}, bf16[2,384,2048,1]{2,1,0,3:T(8,128)(2,1)}, u32[]{:S(2)}) copy-start(bf16[2,384,2048,1]{2,1,0,3:T(8,128)(2,1)} %reshape.113) | copy-start | bytes 9437188
  484.4 3.1 copy-start.1
Sparse Core Ops, SparseCore 0:
  11.2 100.8 all-gather.13
  115.2 106.7 all-gather.11
  223.8 20.6 all-gather.9
  246.2 23.3 all-gather.7
  314.1 67.0 reduce-scatter.1
